TPU v7x, 256 devices: a whole 4x4x8 slice. The times are simulated.
256 devices in a mesh: chan: 128 (over x_lo, z, y, core), tm: 2 (over x_hi).
Axes of the slice: x: 4 (x_hi: 2, x_lo: 2; x = x_hi * 2 + x_lo), y: 4, z: 8, core: 2. Of those that a mesh axis runs over, the one named last changes fastest.
Arguments:
- records: bfloat16 [6, 2048, 16384], P('tm', None, 'chan'), may hold values from -600 to 600
- band_taps: float32 [64], replicated, may hold values from -0.75 to 0.75
- white_taps: float32 [16, 16384], P(None, 'chan'), may hold values from -1.5 to 1.5
- live_mask: int32 [16384], P('chan'), may hold values 0 or 1
- partners: int32 [6, 128], P(None, 'chan'), may hold values from 0 to 127, as said below
Outputs:
- correlations: float32 [6, 32, 16384, 128], P(None, 'tm', 'chan')
Inputs may be any that keep to these rules, and one draw needn't show every extreme that they name: In each round blocks are matched in pairs: partners[r, b] differs from b, partners[r, partners[r, b]] = b, and partners[r, b] - b equals d or -d modulo 128, with the same d in the finite set (1, 2, 4) for all blocks of the round. Over all rounds every block b is matched with b + 1, b - 1, b + 2, b - 2, b + 4 and b - 4 modulo 128, each once.
All inputs are finite; a program needn't handle non-finite values. No bound on the sum of `live_mask` on one device may be relied on, other than what follows from the above.
Results may differ from a plain program's by a relative error of at most 0.0058.
Values may be sent and summed in bfloat16 or wider, within the bound.
No kernel may reach another device: no remote copies, remote signals or barrier semaphores. Data moves between devices by JAX's collectives and lax.ppermute only.
A program may use at most 64 MiB of HBM per device.

v0:
```python
import math

import jax
import jax.numpy as jnp
from jax import lax
from jax.sharding import PartitionSpec as P

NB = 128
SEG = 6
LAGS = 32


def shifted(value, axis, steps):
    count = lax.axis_size(axis)
    pairs = [(source, (source + steps) % count) for source in range(count)]
    return lax.ppermute(value, axis, pairs)


def bin_numbers(samples, bin_count):
    return samples // 64 + samples // (4 * bin_count) * jnp.arange(bin_count, dtype=jnp.int32)


def rotation(products, samples):
    angles = jnp.mod(products, samples).astype(jnp.float32) * (2.0 * math.pi / samples)
    return (jnp.cos(angles), jnp.sin(angles))


def dft_table(samples, bin_index):
    sample_index = jnp.arange(samples, dtype=jnp.int32)
    cos_part, sin_part = rotation(sample_index[:, None] * bin_index[None, :], samples)
    return jnp.concatenate([cos_part, -sin_part], axis=1).astype(jnp.bfloat16)


def responses(band_taps, white_taps, bin_index, samples):
    highest = lax.Precision.HIGHEST
    band_cos, band_sin = rotation(
        jnp.arange(band_taps.shape[0], dtype=jnp.int32)[:, None] * bin_index[None, :], samples
    )
    white_cos, white_sin = rotation(
        jnp.arange(white_taps.shape[0], dtype=jnp.int32)[:, None] * bin_index[None, :], samples
    )
    band_real = jnp.dot(band_taps, band_cos, precision=highest)
    band_imag = -jnp.dot(band_taps, band_sin, precision=highest)
    white_real = jnp.dot(white_taps.T, white_cos, precision=highest)
    white_imag = -jnp.dot(white_taps.T, white_sin, precision=highest)
    resp_real = white_real * band_real[None, :] - white_imag * band_imag[None, :]
    resp_imag = white_real * band_imag[None, :] + white_imag * band_real[None, :]
    return (resp_real, resp_imag)


def filtered(raw_spec, resp_real, resp_imag, live_values):
    bin_count = resp_real.shape[1]
    spec_real = raw_spec[..., :bin_count]
    spec_imag = raw_spec[..., bin_count:]
    real_resp = resp_real[:, None, :]
    imag_resp = resp_imag[:, None, :]
    out_real = (real_resp * spec_real - imag_resp * spec_imag) * live_values[:, None, None]
    out_imag = (real_resp * spec_imag + imag_resp * spec_real) * live_values[:, None, None]
    return jnp.concatenate([out_real, out_imag], axis=2).astype(jnp.bfloat16)


def inverse_norms(flat_rows):
    values = flat_rows.astype(jnp.float32)
    mean_square = jnp.sum(values * values, axis=-1) / (SEG * NB)
    return lax.rsqrt(mean_square + 1e-06)


def turned_rows(own_block, lag_values, bin_index, samples):
    lag_cos, lag_sin = rotation(lag_values[:, None] * bin_index[None, :], samples)
    values = own_block.astype(jnp.float32).reshape(own_block.shape[0], SEG, 2, NB)
    part_real = values[:, :, 0, :][None]
    part_imag = values[:, :, 1, :][None]
    cos_factor = lag_cos[:, None, None, :]
    sin_factor = lag_sin[:, None, None, :]
    new_real = part_real * cos_factor - part_imag * sin_factor
    new_imag = part_real * sin_factor + part_imag * cos_factor
    stacked = jnp.stack([new_real, new_imag], axis=3)
    return stacked.astype(jnp.bfloat16).reshape(lag_values.shape[0] * own_block.shape[0], -1)


def tile_sums(turned, chosen, own_scale, part_scale, lag_count):
    rounds, row_count, inner_size = chosen.shape
    flat_rows = chosen.reshape(rounds * row_count, inner_size)
    tile_totals = lax.dot_general(
        turned, flat_rows, (((1,), (1,)), ((), ())), preferred_element_type=jnp.float32
    )
    tile_totals = tile_totals.reshape(lag_count, row_count, rounds, row_count)
    scaled = (
        tile_totals
        * own_scale[None, :, None, None]
        * part_scale[None, None, :, :]
        * (1.0 / math.sqrt(SEG * NB))
    )
    return jnp.transpose(scaled, (2, 0, 1, 3))


def local(records, band_taps, white_taps, live_mask, partners):
    samples = records.shape[1]
    channels = records.shape[2]
    bin_index = bin_numbers(samples, NB)
    transform = dft_table(samples, bin_index)
    resp_real, resp_imag = responses(band_taps, white_taps, bin_index, samples)
    live_values = live_mask.astype(jnp.float32)
    raw_spec = jnp.einsum(
        "stc,tf->csf",
        lax.all_gather(records, "tm", axis=0, tiled=True),
        transform,
        preferred_element_type=jnp.float32,
    )
    spectra = filtered(raw_spec, resp_real, resp_imag, live_values)
    own_block = spectra.reshape(channels, -1)
    my_block = lax.axis_index("chan")
    block_count = lax.axis_size("chan")
    offset_list = (-4, -2, -1, 1, 2, 4)
    pieces = {}
    for offset in (1, 2, 4, -1, -2, -4):
        pieces[offset] = shifted(own_block, "chan", -offset)
    window = jnp.stack([pieces[offset] for offset in offset_list])
    delta = jnp.mod(partners[:, 0] - my_block + block_count // 2, block_count) - block_count // 2
    slot_index = jnp.zeros_like(delta)
    for position, offset in enumerate(offset_list):
        slot_index = slot_index + position * (delta == offset).astype(jnp.int32)
    chosen = jnp.take(window, slot_index, axis=0)
    own_scale = inverse_norms(own_block)
    part_scale = inverse_norms(chosen)
    lag_count = LAGS // lax.axis_size("tm")
    lag_first = lax.axis_index("tm") * lag_count
    lag_values = 3 * (lag_first + jnp.arange(lag_count, dtype=jnp.int32) - LAGS // 2)
    turned = turned_rows(own_block, lag_values, bin_index, samples)
    return tile_sums(turned, chosen, own_scale, part_scale, lag_count)


def solution(mesh):
    return jax.shard_map(
        local,
        mesh=mesh,
        in_specs=(P("tm", None, "chan"), P(), P(None, "chan"), P("chan"), P(None, "chan")),
        out_specs=P(None, "tm", "chan", None),
        check_vma=False,
    )
```

profile of v0, /device:TPU:1, one launch (start us, length us, event | category | flops | bytes accessed | tf_op | source)
XLA Modules:
  0.0 153.3 jit_solution(10691760521809553635)
XLA Ops:
  6.5 0.0 copy-start
  6.5 0.0 all-gather.2.cloned.1.call-start
  6.5 0.7 all-gather.2.cloned.1.call-update
  7.3 0.7 convert_element_type.73
  7.9 0.7 and_bitcast_fusion
  8.6 0.9 convolution_bitcast_fusion.2
  9.6 0.9 fusion.5
  10.5 0.1 fusion.39
  10.6 0.0 copy-done
  10.7 0.3 convolution_negate_fusion
  11.0 0.3 subtract_bitcast_fusion
  11.4 4.9 %cosine_convert_fusion = (bf16[2048,128]{0,1:T(8,128)(2,1)S(1)}, bf16[2048,128]{0,1:T(8,128)(2,1)S(1)}) fusion(s32[128]{0:T(128)S(1)} %multiply_add_fusion), kind=kLoop, calls=%fused_computation.25 | loop fusion | flops 4456448 | bytes 1049088 | tf_op jit(solution)/shard_map/convert.3
  16.2 48.3 %all-gather.2.cloned.1.call-done = bf16[6,2048,128]{2,1,0:T(8,128)(2,1)} async-done(((bf16[3,2048,128]{2,1,0:T(8,128)(2,1)}), bf16[6,2048,128]{2,1,0:T(8,128)(2,1)}) %all-gather.2.cloned.1.call-update) | async-done | bytes 3145744 | tf_op jit(solution)/shard_map/all_gather | solution.py:106
  64.5 2.9 %convolution_bitcast_fusion = f32[128,6,256]{0,2,1:T(8,128)S(1)} fusion(bf16[6,2048,128]{2,1,0:T(8,128)(2,1)} %all-gather.2.cloned.1.call-done, bf16[2048,128]{0,1:T(8,128)(2,1)S(1)} %get-tuple-element.20, bf16[2048,128]{0,1:T(8,128)(2,1)S(1)} %get-tuple-element.19), kind=kOutput, calls=%fused_computation.13 | convolution fusion | flops 807403520 | bytes 4980736 | tf_op jit(solution)/shard_map/stc,tf->csf/dot_general | solution.py:104
  67.4 0.1 subtract_multiply_fusion
  67.5 0.2 multiply_reduce_fusion.1
  67.7 0.2 copy.20
  67.9 2.8 %collective-permute-start = (bf16[128,1536]{1,0:T(8,128)(2,1)S(1)}, bf16[128,1536]{1,0:T(8,128)(2,1)}, u32[]{:S(2)}, u32[]{:S(2)}) collective-permute-start(bf16[128,1536]{1,0:T(8,128)(2,1)S(1)} %copy.20), channel_id=1, source_target_pairs={{0,8},{2,10},{4,12},{6,14},{8,16},{10,18},{12,20},{14,22},{16,24},... | collective-permute-start | bytes 1179656 | tf_op jit(solution)/shard_map/ppermute | solution.py:16
  70.7 0.3 collective-permute-start.1
  71.0 1.7 %collective-permute-start.2 = (bf16[128,1536]{1,0:T(8,128)(2,1)S(1)}, bf16[128,1536]{1,0:T(8,128)(2,1)S(1)}, u32[]{:S(2)}, u32[]{:S(2)}) collective-permute-start(bf16[128,1536]{1,0:T(8,128)(2,1)S(1)} %copy.20), channel_id=1, source_target_pairs={{0,2},{2,4},{4,6},{6,8},{8,10},{10,12},{12,14},{14,16},{16,18},{18... | collective-permute-start | bytes 1179656 | tf_op jit(solution)/shard_map/ppermute | solution.py:16
  72.8 0.0 collective-permute-start.3
  72.8 5.1 %collective-permute-start.4 = (bf16[128,1536]{1,0:T(8,128)(2,1)S(1)}, bf16[128,1536]{1,0:T(8,128)(2,1)S(1)}, u32[]{:S(2)}, u32[]{:S(2)}) collective-permute-start(bf16[128,1536]{1,0:T(8,128)(2,1)S(1)} %copy.20), channel_id=1, source_target_pairs={{0,252},{2,254},{4,0},{6,2},{8,4},{10,6},{12,8},{14,10},{16,12},{1... | collective-permute-start | bytes 1179656 | tf_op jit(solution)/shard_map/ppermute | solution.py:16
  77.9 0.1 convert.22
  78.0 0.1 slice_bitcast_fusion.1
  78.0 0.2 copy.18
  78.3 0.2 copy.19
  78.5 13.2 %subtract_convert_fusion = (bf16[16,128,6,1,128]{4,3,2,1,0:T(2,128)(2,1)S(1)}, bf16[16,128,6,1,128]{4,3,2,1,0:T(2,128)(2,1)S(1)}) fusion(f32[16,128]{1,0:T(8,128)S(1)} %get-tuple-element.18, f32[128,6,128]{2,1,0:T(8,128)S(1)} %copy.19, f32[16,128]{1,0:T(8,128)S(1)} %get-tuple-element.17, f32[128,6,128]{2,1,0:T(8,128)S(1)} %copy.18), kind=kLoop, calls=%fused_computation.6 | loop fusion | flops 12582912 | bytes 7094272 | tf_op jit(solution)/shard_map/convert.1
  91.7 15.4 %pad_maximum_fusion = bf16[16,128,6,2,128]{4,3,2,1,0:T(2,128)(2,1)} fusion(bf16[16,128,6,1,128]{4,3,2,1,0:T(2,128)(2,1)S(1)} %get-tuple-element.10, bf16[16,128,6,1,128]{4,3,2,1,0:T(2,128)(2,1)S(1)} %get-tuple-element.9), kind=kLoop, calls=%fused_computation.1 | loop fusion | flops 12582912 | bytes 12582912 | tf_op jit(solution)/shard_map/stack | solution.py:77
  107.1 14.4 %reshape.152 = bf16[16,128,1536,1]{2,1,0,3:T(8,128)(2,1)} reshape(bf16[16,128,6,2,128]{4,3,2,1,0:T(2,128)(2,1)} %pad_maximum_fusion) | data formatting | bytes 12582912 | tf_op jit(solution)/shard_map/convert_element_type | solution.py:78
  121.5 0.0 collective-permute-done
  121.5 1.1 collective-permute-start.5
  122.6 1.8 %bitcast_dynamic-update-slice_fusion.5 = bf16[6,128,1536]{2,1,0:T(8,128)(2,1)} fusion(bf16[128,1536]{1,0:T(8,128)(2,1)} %collective-permute-done), kind=kLoop, calls=%fused_computation.38 | loop fusion | bytes 786432
  124.4 0.0 collective-permute-done.1
  124.4 0.8 bitcast_dynamic-update-slice_fusion.4
  125.2 0.0 collective-permute-done.2
  125.2 0.8 bitcast_dynamic-update-slice_fusion.3
  125.9 0.0 collective-permute-done.3
  125.9 0.8 bitcast_dynamic-update-slice_fusion.2
  126.7 0.0 collective-permute-done.4
  126.7 0.8 bitcast_dynamic-update-slice_fusion.1
  127.5 4.6 %collective-permute-done.5 = bf16[128,1536]{1,0:T(8,128)(2,1)S(1)} collective-permute-done((bf16[128,1536]{1,0:T(8,128)(2,1)S(1)}, bf16[128,1536]{1,0:T(8,128)(2,1)S(1)}, u32[]{:S(2)}, u32[]{:S(2)}) %collective-permute-start.5) | collective-permute-done | bytes 393248 | tf_op jit(solution)/shard_map/ppermute | solution.py:16
  132.1 0.8 bitcast_dynamic-update-slice_fusion
  132.9 2.4 %gather_fusion = bf16[6,128,1536]{2,1,0:T(8,128)(2,1)S(1)} fusion(bf16[6,128,1536]{2,1,0:T(8,128)(2,1)} %bitcast_dynamic-update-slice_fusion, s32[1024]{0:T(1024)S(1)} %pad_clamp_fusion), kind=kCustom, calls=%fused_computation | custom fusion | bytes 4718616 | tf_op jit(solution)/shard_map/jit(_take)/gather | solution.py:123
  135.2 0.8 multiply_reduce_fusion
  136.0 7.4 %multiply_bitcast_fusion = f32[6,16,128,128]{3,2,0,1:T(8,128)S(1)} fusion(f32[6,128]{1,0:T(8,128)S(1)} %add_rsqrt_fusion, f32[128]{0:T(128)S(1)} %add_rsqrt_fusion.1, bf16[16,128,1536,1]{2,1,0,3:T(8,128)(2,1)} %reshape.152, bf16[6,128,1536]{2,1,0:T(8,128)(2,1)S(1)} %gather_fusion, pred[6]{0:T(512)(128)(4,1)S(1)} %get-tuple-element.7), kind=kOutput, calls=%fused_computation.4 | convolution fusion | flops 4837736448 | bytes 14945798 | tf_op jit(solution)/shard_map/dot_general | solution.py:84
  143.4 3.1 %copy.26 = f32[6,16,128,128]{3,2,1,0:T(8,128)} copy(f32[6,16,128,128]{3,2,0,1:T(8,128)S(1)} %multiply_bitcast_fusion) | data formatting | bytes 12582912 | tf_op jit(solution)/shard_map/mul | solution.py:89
  (5 shorter events, 0.0 us)
Async XLA Ops:
  6.5 4.1 %copy-start = (f32[16,128]{1,0:T(8,128)S(1)}, f32[16,128]{1,0:T(8,128)}, u32[]{:S(2)}) copy-start(f32[16,128]{1,0:T(8,128)} %param.7) | copy-start | bytes 24580
  6.5 58.0 %all-gather.2.cloned.1.call-start = ((), (), s32[]{:S(2)}) async-start(), calls=%async_computation | async-start | bytes 4718592 | tf_op jit(solution)/shard_map/all_gather | solution.py:106
  67.9 53.6 %collective-permute-start = (bf16[128,1536]{1,0:T(8,128)(2,1)S(1)}, bf16[128,1536]{1,0:T(8,128)(2,1)}, u32[]{:S(2)}, u32[]{:S(2)}) collective-permute-start(bf16[128,1536]{1,0:T(8,128)(2,1)S(1)} %copy.20), channel_id=1, source_target_pairs={{0,8},{2,10},{4,12},{6,14},{8,16},{10,18},{12,20},{14,22},{16,24},... | collective-permute-start | bytes 1179656 | tf_op jit(solution)/shard_map/ppermute | solution.py:16
  70.7 53.7 %collective-permute-start.1 = (bf16[128,1536]{1,0:T(8,128)(2,1)S(1)}, bf16[128,1536]{1,0:T(8,128)(2,1)S(1)}, u32[]{:S(2)}, u32[]{:S(2)}) collective-permute-start(bf16[128,1536]{1,0:T(8,128)(2,1)S(1)} %copy.20), channel_id=1, source_target_pairs={{0,4},{2,6},{4,8},{6,10},{8,12},{10,14},{12,16},{14,18},{16,20},{1... | collective-permute-start | bytes 1179656 | tf_op jit(solution)/shard_map/ppermute | solution.py:16
  71.0 54.1 %collective-permute-start.2 = (bf16[128,1536]{1,0:T(8,128)(2,1)S(1)}, bf16[128,1536]{1,0:T(8,128)(2,1)S(1)}, u32[]{:S(2)}, u32[]{:S(2)}) collective-permute-start(bf16[128,1536]{1,0:T(8,128)(2,1)S(1)} %copy.20), channel_id=1, source_target_pairs={{0,2},{2,4},{4,6},{6,8},{8,10},{10,12},{12,14},{14,16},{16,18},{18... | collective-permute-start | bytes 1179656 | tf_op jit(solution)/shard_map/ppermute | solution.py:16
  72.8 53.2 %collective-permute-start.3 = (bf16[128,1536]{1,0:T(8,128)(2,1)S(1)}, bf16[128,1536]{1,0:T(8,128)(2,1)S(1)}, u32[]{:S(2)}, u32[]{:S(2)}) collective-permute-start(bf16[128,1536]{1,0:T(8,128)(2,1)S(1)} %copy.20), channel_id=1, source_target_pairs={{0,254},{2,0},{4,2},{6,4},{8,6},{10,8},{12,10},{14,12},{16,14},{18... | collective-permute-start | bytes 1179656 | tf_op jit(solution)/shard_map/ppermute | solution.py:16
  72.8 53.9 %collective-permute-start.4 = (bf16[128,1536]{1,0:T(8,128)(2,1)S(1)}, bf16[128,1536]{1,0:T(8,128)(2,1)S(1)}, u32[]{:S(2)}, u32[]{:S(2)}) collective-permute-start(bf16[128,1536]{1,0:T(8,128)(2,1)S(1)} %copy.20), channel_id=1, source_target_pairs={{0,252},{2,254},{4,0},{6,2},{8,4},{10,6},{12,8},{14,10},{16,12},{1... | collective-permute-start | bytes 1179656 | tf_op jit(solution)/shard_map/ppermute | solution.py:16
  121.5 10.6 %collective-permute-start.5 = (bf16[128,1536]{1,0:T(8,128)(2,1)S(1)}, bf16[128,1536]{1,0:T(8,128)(2,1)S(1)}, u32[]{:S(2)}, u32[]{:S(2)}) collective-permute-start(bf16[128,1536]{1,0:T(8,128)(2,1)S(1)} %copy.20), channel_id=1, source_target_pairs={{0,248},{2,250},{4,252},{6,254},{8,0},{10,2},{12,4},{14,6},{16,8},... | collective-permute-start | bytes 1179656 | tf_op jit(solution)/shard_map/ppermute | solution.py:16
Sparse Core Ops, SparseCore 0:
  9.2 55.3 all-gather.1
where the time goes:
time: 154 us; the launch traced here: 153 us
  waiting for transfers between devices  53.6 us (35%)
  other arithmetic  36.1 us (23%)
  local copies, waits for them, and re-layouts  26.2 us (17%)
  between operations  13.5 us (9%)
  matrix products  12.8 us (8%)
  starting transfers between devices  11.1 us (7%)
    all_gather x1, waiting for transfers between devices, local(): lax.all_gather(records, 'tm', axis=0, tiled=True)  48.3 us
    another operation x2, other arithmetic  18.1 us
    another operation x1, other arithmetic, turned_rows(): stacked = jnp.stack([new_real, new_imag], axis=3)  15.4 us
    convert_element_type x1, local copies, waits for them, and re-layouts, turned_rows(): stacked.astype(jnp.bfloat16)  14.4 us
    ppermute x6, starting transfers between devices, shifted(): return lax.ppermute(value, axis, pairs)  11.1 us
    dot_general x1, matrix products, tile_sums(): lax.dot_general(turned, flat_rows, (((1,), (1,)), ((), ())), preferred_el...  7.36 us
    unnamed x7, local copies, waits for them, and re-layouts  4.86 us
    ppermute x6, waiting for transfers between devices, shifted(): return lax.ppermute(value, axis, pairs)  4.6 us
  transfers between devices with their start and end apart: 7, of which 2 were waited for; matrix products, arithmetic and copies ran while one was open for 37% of the time, Pallas kernels for 0%

commit v1 on v0

v1 whole, which is shorter than its diff:
```python
import functools
import math

import jax
import jax.numpy as jnp
import ml_dtypes
import numpy as np
from jax import lax
from jax.experimental import pallas as pl
from jax.experimental.pallas import tpu as pltpu
from jax.sharding import PartitionSpec as P

NB = 128
SEG = 6
LAGS = 32
ROUNDS = 6
CHUNK = 256


def angles(products, samples):
    return np.mod(products, samples).astype(np.float32) * np.float32(2.0 * math.pi / samples)


def tables(samples, band_count, white_count, half_lags):
    bins = (samples // 64 + samples // (4 * NB) * np.arange(NB)).astype(np.int64)
    period = samples // math.gcd(samples, int(np.gcd.reduce(bins)))
    wave = angles(bins[:, None] * np.arange(period)[None, :], samples)
    dft = np.concatenate([np.cos(wave), -np.sin(wave)], axis=0).astype(ml_dtypes.bfloat16)
    band = angles(bins[:, None] * np.arange(band_count)[None, :], samples)
    white = angles(bins[:, None] * np.arange(white_count)[None, :], samples)
    lag_values = 3 * (np.arange(LAGS) - LAGS // 2)
    lag = angles(lag_values[:, None] * bins[None, :], samples)
    lag_table = np.stack([np.cos(lag), np.sin(lag)], axis=0).astype(np.float32)
    lag_table = lag_table.reshape(2, LAGS // half_lags, half_lags, 1, NB).transpose(1, 0, 2, 3, 4)
    return (
        dft,
        np.stack([np.cos(band), -np.sin(band)]).astype(np.float32),
        np.concatenate([np.cos(white), -np.sin(white)], axis=0).astype(np.float32),
        lag_table,
    )


def spectra_kernel(
    rec_hbm, dft_hbm, band_hbm, white_hbm, band_taps, white_taps, live_hbm, out_ref,
    rec_ref, dft_ref, band_table, white_table, band_ref, white_ref, live_ref, sems, rec_sems,
):
    segments, samples, channels = rec_ref.shape
    small = [
        (band_hbm, band_table),
        (white_hbm, white_table),
        (band_taps, band_ref),
        (white_taps, white_ref),
        (live_hbm, live_ref),
        (dft_hbm, dft_ref),
    ]
    copies = [pltpu.make_async_copy(a, b, sems.at[k]) for k, (a, b) in enumerate(small)]
    loads = [
        pltpu.make_async_copy(rec_hbm.at[seg], rec_ref.at[seg], rec_sems.at[seg])
        for seg in range(segments)
    ]
    for copy in copies + loads:
        copy.start()
    for copy in copies:
        copy.wait()
    band = band_ref[...]
    band_real = jnp.sum(band_table[0] * band, axis=1, keepdims=True)
    band_imag = jnp.sum(band_table[1] * band, axis=1, keepdims=True)
    white = jnp.dot(
        white_table[...],
        white_ref[...],
        precision=lax.Precision.HIGHEST,
        preferred_element_type=jnp.float32,
    )
    white_real, white_imag = white[:NB], white[NB:]
    live = live_ref[...].astype(jnp.float32)
    resp_real = white_real * band_real - white_imag * band_imag
    resp_imag = white_real * band_imag + white_imag * band_real
    period = dft_ref.shape[1]
    for seg in range(segments):
        loads[seg].wait()
        parts = [rec_ref[seg, k * period : (k + 1) * period, :] for k in range(samples // period)]
        wide = jnp.dot(
            dft_ref[...], jnp.concatenate(parts, axis=1), preferred_element_type=jnp.float32
        )
        raw = wide[:, :channels]
        for k in range(1, len(parts)):
            raw = raw + wide[:, k * channels : (k + 1) * channels]
        raw_real, raw_imag = raw[:NB], raw[NB:]
        real = (resp_real * raw_real - resp_imag * raw_imag) * live
        imag = (resp_real * raw_imag + resp_imag * raw_real) * live
        row = seg * 2 * NB
        out_ref[row : row + NB, :] = real.astype(jnp.bfloat16)
        out_ref[row + NB : row + 2 * NB, :] = imag.astype(jnp.bfloat16)


def turn_kernel(own_ref, other_ref, lag_ref, turned_ref, scale_ref, rows_ref):
    half = own_ref.shape[0]
    channels = own_ref.shape[1]
    for index, ref in enumerate((own_ref, other_ref)):
        for k in range(0, half, NB):
            tile = ref[k : k + NB, :].astype(jnp.float32)
            rows_ref[:, index * half + k : index * half + k + NB] = tile.T
    values = rows_ref[...]
    mean_square = jnp.sum(values * values, axis=1, keepdims=True) / (SEG * NB)
    scale_ref[...] = jnp.broadcast_to(lax.rsqrt(mean_square + 1e-06), scale_ref.shape)

    def one_lag(lag, carry):
        cos_factor = lag_ref[0, lag]
        sin_factor = lag_ref[1, lag]
        start = pl.multiple_of(lag * channels, channels)
        for k in range(0, 2 * half, 2 * NB):
            real = rows_ref[:, k : k + NB]
            imag = rows_ref[:, k + NB : k + 2 * NB]
            new_real = real * cos_factor - imag * sin_factor
            new_imag = real * sin_factor + imag * cos_factor
            turned_ref[pl.ds(start, channels), k : k + NB] = new_real.astype(jnp.bfloat16)
            turned_ref[pl.ds(start, channels), k + NB : k + 2 * NB] = new_imag.astype(jnp.bfloat16)
        return carry

    lax.fori_loop(0, lag_ref.shape[1], one_lag, 0)


def column_scale(first, second):
    total = jnp.zeros((1, first.shape[1]), jnp.float32)
    for part in (first, second):
        values = part[...].astype(jnp.float32)
        total = total + jnp.sum(values * values, axis=0, keepdims=True)
    return lax.rsqrt(total / (SEG * NB) + 1e-06)


def pair_kernel(half, rows_at, slot_ref, turned_ref, scale_ref, *rest):
    out_ref, stage, sems = rest[-3:]
    channels = scale_ref.shape[0]
    ah, ao, bh, bo = [ref.at[at : at + half] for ref, at in zip(rest[:4], rows_at)]
    near = jnp.concatenate([ah[...], bh[...]], axis=1)
    far = jnp.concatenate([ao[...], bo[...]], axis=1)
    rows = turned_ref.shape[0]
    lags = CHUNK // channels
    copies = []
    for chunk in range(rows // CHUNK):
        start = chunk * CHUNK
        totals = jnp.dot(
            turned_ref[start : start + CHUNK, :half], near, preferred_element_type=jnp.float32
        ) + jnp.dot(
            turned_ref[start : start + CHUNK, half:], far, preferred_element_type=jnp.float32
        )
        if chunk == 0:
            own = scale_ref[...] * (1.0 / math.sqrt(SEG * NB))
            scales = [own * column_scale(ah, ao), own * column_scale(bh, bo)]
        for lag in range(lags):
            row = lag * channels
            for side in range(2):
                stage[side, chunk * lags + lag] = (
                    totals[row : row + channels, side * channels : (side + 1) * channels]
                    * scales[side]
                )
        for side in range(2):
            copy = pltpu.make_async_copy(
                stage.at[side, pl.ds(chunk * lags, lags)],
                out_ref.at[slot_ref[side], pl.ds(chunk * lags, lags)],
                sems.at[side, chunk],
            )
            copy.start()
            copies.append(copy)
    for copy in copies:
        copy.wait()


VMEM = pl.BlockSpec(memory_space=pltpu.VMEM)


def own_spectra(records, band_taps, white_taps, live_mask, consts):
    segments, samples, channels = records.shape
    dft, band_table, white_table = consts
    return pl.pallas_call(
        spectra_kernel,
        out_shape=jax.ShapeDtypeStruct((segments * 2 * NB, channels), jnp.bfloat16),
        in_specs=[pl.BlockSpec(memory_space=pltpu.HBM)] * 7,
        out_specs=VMEM,
        scratch_shapes=[
            pltpu.VMEM(records.shape, records.dtype),
            pltpu.VMEM(dft.shape, dft.dtype),
            pltpu.VMEM(band_table.shape, jnp.float32),
            pltpu.VMEM(white_table.shape, jnp.float32),
            pltpu.VMEM((1, band_taps.shape[0]), jnp.float32),
            pltpu.VMEM(white_taps.shape, jnp.float32),
            pltpu.VMEM((1, channels), jnp.int32),
            pltpu.SemaphoreType.DMA((6,)),
            pltpu.SemaphoreType.DMA((segments,)),
        ],
        name="spectra",
        compiler_params=pltpu.CompilerParams(vmem_limit_bytes=60 << 20),
        cost_estimate=pl.CostEstimate(
            flops=2 * segments * samples * channels * 2 * NB,
            bytes_accessed=2 * segments * samples * channels,
            transcendentals=0,
        ),
    )(
        records,
        dft,
        band_table,
        white_table,
        band_taps.reshape(1, -1),
        white_taps,
        live_mask.reshape(1, -1),
    )


def turned_rows(own, other, lag_table):
    half, channels = own.shape
    lag_count = lag_table.shape[1]
    return pl.pallas_call(
        turn_kernel,
        out_shape=(
            jax.ShapeDtypeStruct((lag_count * channels, 2 * half), jnp.bfloat16),
            jax.ShapeDtypeStruct((channels, channels), jnp.float32),
        ),
        in_specs=[VMEM] * 3,
        out_specs=(VMEM, VMEM),
        scratch_shapes=[pltpu.VMEM((channels, 2 * half), jnp.float32)],
        name="turn",
        compiler_params=pltpu.CompilerParams(vmem_limit_bytes=24 << 20),
    )(own, other, lag_table)


def pair_sums(slots, turned, scale, first, second, lag_count, previous):
    channels = scale.shape[0]
    half = turned.shape[1] // 2
    pieces = [*first, *second]
    operands = [slots, turned, scale] + [array for array, _ in pieces]
    specs = [pl.BlockSpec(memory_space=pltpu.SMEM)] + [VMEM] * 6
    aliases = {}
    if previous is not None:
        aliases = {len(operands): 0}
        operands.append(previous)
        specs.append(pl.BlockSpec(memory_space=pl.ANY))
    return pl.pallas_call(
        functools.partial(pair_kernel, half, [at for _, at in pieces]),
        out_shape=jax.ShapeDtypeStruct((ROUNDS, lag_count, channels, channels), jnp.float32),
        in_specs=specs,
        out_specs=pl.BlockSpec(memory_space=pl.ANY),
        scratch_shapes=[
            pltpu.VMEM((2, lag_count, channels, channels), jnp.float32),
            pltpu.SemaphoreType.DMA((2, lag_count * channels // CHUNK)),
        ],
        input_output_aliases=aliases,
        name="pair",
        compiler_params=pltpu.CompilerParams(vmem_limit_bytes=24 << 20),
    )(*operands)


def shifted(value, steps):
    count = lax.axis_size("chan")
    return lax.ppermute(value, "chan", [(s, (s + steps) % count) for s in range(count)])


def neighbour(value):
    return lax.ppermute(value, "chan", [(s, s ^ 1) for s in range(lax.axis_size("chan"))])


def mirrored(value):
    return lax.ppermute(value, "tm", [(0, 1), (1, 0)])


def local(consts, records, band_taps, white_taps, live_mask, partners):
    lag_count = LAGS // lax.axis_size("tm")
    my_block = lax.axis_index("chan")
    block_count = lax.axis_size("chan")
    is_odd = my_block % 2 == 1
    half = own_spectra(records, band_taps, white_taps, live_mask, consts[:3])

    delta = jnp.mod(partners[:, 0] - my_block + block_count // 2, block_count) - block_count // 2
    inner = jnp.where(is_odd, -1, 1)
    two = jnp.full_like(inner, 2)
    offsets = jnp.stack([-two, two, inner, -inner, -2 * two, 2 * two])
    rounds = jnp.arange(ROUNDS, dtype=jnp.int32)
    slots = jnp.sum(
        jnp.where(delta[None, :] == offsets[:, None], rounds[None, :], 0), axis=1
    ).astype(jnp.int32)
    lag_table = lax.dynamic_index_in_dim(consts[3], lax.axis_index("tm"), 0, keepdims=False)

    far = mirrored(half)
    low2, high2 = shifted(half, 2), shifted(half, -2)
    chip = neighbour(half)
    far, low2, high2, chip = lax.optimization_barrier((far, low2, high2, chip))
    both_far = mirrored(jnp.concatenate([low2, high2], axis=0))
    mixed = neighbour(jnp.concatenate([far, jnp.where(is_odd, low2, high2)], axis=0))
    low4, high4 = shifted(low2, 2), shifted(high2, -2)
    low4_far, high4_far = shifted(far, 4), shifted(far, -4)
    turned, scale = turned_rows(half, far, lag_table)
    size = half.shape[0]
    sent = jnp.where(is_odd, both_far[:size], both_far[size:])
    sent, turned = lax.optimization_barrier((sent, turned))
    across_far = neighbour(sent)

    near2 = ((low2, 0), (both_far, 0)), ((high2, 0), (both_far, size))
    near1 = ((chip, 0), (mixed, 0)), ((mixed, size), (across_far, 0))
    near4 = ((low4, 0), (low4_far, 0)), ((high4, 0), (high4_far, 0))
    out = pair_sums(slots[0:2], turned, scale, *near2, lag_count, None)
    out = pair_sums(slots[2:4], turned, scale, *near1, lag_count, out)
    return pair_sums(slots[4:6], turned, scale, *near4, lag_count, out)


def solution(mesh):
    def whole(records, band_taps, white_taps, live_mask, partners):
        consts = tables(
            records.shape[1], band_taps.shape[0], white_taps.shape[0], LAGS // mesh.shape["tm"]
        )
        return jax.shard_map(
            functools.partial(local, consts),
            mesh=mesh,
            in_specs=(P("tm", None, "chan"), P(), P(None, "chan"), P("chan"), P(None, "chan")),
            out_specs=P(None, "tm", "chan", None),
            check_vma=False,
        )(records, band_taps, white_taps, live_mask, partners)

    return whole
```

time: 154 us -> 48 us (0.31)
  waiting for transfers between devices: 53.6 us -> 2.76 us
  other arithmetic: 36.1 us -> 0.95 us
  local copies, waits for them, and re-layouts: 26.2 us -> 1.8 us
  Pallas kernels: 0 us -> 15.7 us
  starting transfers between devices: 11.1 us -> 26.3 us
  between operations: 13.5 us -> 0.29 us
  matrix products: 12.8 us -> 0 us
    all_gather x1 -> x0, waiting for transfers between devices: 48.3 us -> none  [local(): lax.all_gather(records, 'tm', axis=0, tiled=True)]
    another operation x3 -> x0, other arithmetic: 33.5 us -> none
    pallas_call x0 -> x5, Pallas kernels: none -> 15.7 us  [the longest x3 10.1 us: pair_sums(): pl.pallas_call(functools.partial(pair_kernel, half, [at for _, at in piec...]
    ppermute x6 -> x11, starting transfers between devices: 11.1 us -> 26.3 us  [the longest x6 16.2 us: shifted(): lax.ppermute(value, 'chan', [(s, (s + steps) % count) for s in range(coun...]
    convert_element_type x2 -> x0, local copies, waits for them, and re-layouts: 14.6 us -> none  [the longest x1 14.4 us: turned_rows(): stacked.astype(jnp.bfloat16)]
    dot_general x6 -> x0, matrix products: 12.8 us -> none  [the longest x1 7.36 us: tile_sums(): lax.dot_general(turned, flat_rows, (((1,), (1,)), ((), ())), preferred_el...]
    unnamed x7 -> x2, local copies, waits for them, and re-layouts: 4.86 us -> 0.93 us
    mul x4 -> x0, local copies, waits for them, and re-layouts: 3.65 us -> none  [the longest x1 3.13 us: tile_sums(): tile_totals * own_scale[None, :, None, None] * part_scale[None, None, :, :]]
  transfers between devices with their start and end apart: 7 -> 11, of which waited for: 2 -> 2; matrix products, arithmetic and copies ran while one was open for 37% -> 4% of each run, Pallas kernels for 0% -> 18%
where the time goes in v1:
time: 48 us; the launch traced here: 47.8 us
  starting transfers between devices  26.3 us (55%)
  Pallas kernels  15.7 us (33%)
  waiting for transfers between devices  2.76 us (6%)
  local copies, waits for them, and re-layouts  1.8 us (4%)
  other arithmetic  0.95 us (2%)
    ppermute x6, starting transfers between devices, shifted(): lax.ppermute(value, 'chan', [(s, (s + steps) % count) for s in range(coun...  16.2 us
    pallas_call x3, Pallas kernels, pair_sums(): pl.pallas_call(functools.partial(pair_kernel, half, [at for _, at in piec...  10.1 us
    ppermute x2, starting transfers between devices, mirrored(): return lax.ppermute(value, 'tm', [(0, 1), (1, 0)])  5.48 us
    ppermute x3, starting transfers between devices, neighbour(): lax.ppermute(value, 'chan', [(s, s ^ 1) for s in range(lax.axis_size('cha...  4.56 us
    pallas_call x1, Pallas kernels, own_spectra(): pl.pallas_call(spectra_kernel, out_shape=jax.ShapeDtypeStruct((segments *...  3.61 us
    ppermute x6, waiting for transfers between devices, shifted(): lax.ppermute(value, 'chan', [(s, (s + steps) % count) for s in range(coun...  2.74 us
    pallas_call x1, Pallas kernels, turned_rows(): pl.pallas_call(turn_kernel, out_shape=(jax.ShapeDtypeStruct((lag_count *...  1.99 us
  transfers between devices with their start and end apart: 11, of which 2 were waited for; matrix products, arithmetic and copies ran while one was open for 4% of the time, Pallas kernels for 18%

profile of v1, /device:TPU:1, one launch (start us, length us, event | category | flops | bytes accessed | tf_op | source)
XLA Modules:
  0.0 47.8 jit_solution(6247564027962622871)
XLA Ops:
  0.0 3.6 %spectra.1.own_ref = bf16[768,128]{1,0:T(8,128)(2,1)} custom-call(bf16[3,2048,128]{2,1,0:T(8,128)(2,1)} %rec_hbm.1, bf16[256,512]{1,0:T(8,128)(2,1)} %constant.63.clone.dft_hbm, f32[2,128,64]{2,1,0:T(8,128)} %constant.64.clone.band_hbm, f32[256,16]{1,0:T(8,128)} %constant.65.clone.white_hbm, f32[1,64]{1,0:T(1,128)} %bitcast.8, f32[16,128]{1,0:T(8,128)} %white_taps.1, ...), custom_call_target="tpu_custom_call" | custom-call | flops 402653184 | bytes 1572864 | tf_op jit(solution)/shard_map/spectra/pallas_call | solution.py:175
  3.6 3.7 %collective-permute-start = (bf16[768,128]{1,0:T(8,128)(2,1)}, bf16[768,128]{1,0:T(8,128)(2,1)S(1)}, u32[]{:S(2)}, u32[]{:S(2)}) collective-permute-start(bf16[768,128]{1,0:T(8,128)(2,1)} %spectra.1.own_ref), channel_id=1, source_target_pairs={{0,1},{1,0},{2,3},{3,2},{4,5},{5,4},{6,7},{7,6},{8,9},{9,8},{10,11... | collective-permute-start | bytes 589832 | tf_op jit(solution)/shard_map/ppermute | solution.py:262
  7.3 1.3 %collective-permute-start.1 = (bf16[768,128]{1,0:T(8,128)(2,1)}, bf16[768,128]{1,0:T(8,128)(2,1)S(1)}, u32[]{:S(2)}, u32[]{:S(2)}) collective-permute-start(bf16[768,128]{1,0:T(8,128)(2,1)} %spectra.1.own_ref), channel_id=1, source_target_pairs={{0,4},{2,6},{4,8},{6,10},{8,12},{10,14},{12,16},{14,18},{16,20},{1... | collective-permute-start | bytes 589832 | tf_op jit(solution)/shard_map/ppermute | solution.py:254
  8.6 6.8 %collective-permute-start.2 = (bf16[768,128]{1,0:T(8,128)(2,1)}, bf16[768,128]{1,0:T(8,128)(2,1)S(1)}, u32[]{:S(2)}, u32[]{:S(2)}) collective-permute-start(bf16[768,128]{1,0:T(8,128)(2,1)} %spectra.1.own_ref), channel_id=1, source_target_pairs={{0,252},{2,254},{4,0},{6,2},{8,4},{10,6},{12,8},{14,10},{16,12},{1... | collective-permute-start | bytes 589832 | tf_op jit(solution)/shard_map/ppermute | solution.py:254
  15.3 1.2 %collective-permute-start.3 = (bf16[768,128]{1,0:T(8,128)(2,1)}, bf16[768,128]{1,0:T(8,128)(2,1)S(1)}, u32[]{:S(2)}, u32[]{:S(2)}) collective-permute-start(bf16[768,128]{1,0:T(8,128)(2,1)} %spectra.1.own_ref), channel_id=1, source_target_pairs={{0,2},{2,0},{4,6},{6,4},{8,10},{10,8},{12,14},{14,12},{16,18},{18,... | collective-permute-start | bytes 589832 | tf_op jit(solution)/shard_map/ppermute | solution.py:258
  16.6 0.7 %fusion = s32[6]{0:T(128)S(1)} fusion(s32[6,1]{0,1:T(1,128)} %param.13, s32[]{:T(128)S(6)} %axis_index.23), kind=kLoop, calls=%fused_computation.8 | loop fusion | flops 84 | bytes 52 | tf_op jit(solution)/shard_map/sub | solution.py:272
  17.2 0.0 collective-permute-done.other_ref
  17.2 2.6 %collective-permute-done.1.rest_0_ = bf16[768,128]{1,0:T(8,128)(2,1)S(1)} collective-permute-done((bf16[768,128]{1,0:T(8,128)(2,1)}, bf16[768,128]{1,0:T(8,128)(2,1)S(1)}, u32[]{:S(2)}, u32[]{:S(2)}) %collective-permute-start.1) | collective-permute-done | bytes 196640 | tf_op jit(solution)/shard_map/ppermute | solution.py:254
  19.9 0.0 collective-permute-done.2.rest_2_
  19.9 0.0 collective-permute-done.3.rest_0_
  19.9 1.8 %collective-permute-start.4 = (bf16[1536,128]{1,0:T(8,128)(2,1)S(1)}, bf16[1536,128]{1,0:T(8,128)(2,1)S(1)}, u32[]{:S(2)}, u32[]{:S(2)}) collective-permute-start(bf16[1536,128]{1,0:T(8,128)(2,1)S(1)} %pad_maximum_fusion), channel_id=1, source_target_pairs={{0,1},{1,0},{2,3},{3,2},{4,5},{5,4},{6,7},{7,6},{8,9},{9,8},{10,11... | collective-permute-start | bytes 1179656 | tf_op jit(solution)/shard_map/ppermute | solution.py:262
  21.8 1.9 %collective-permute-start.9 = (bf16[1536,128]{1,0:T(8,128)(2,1)S(1)}, bf16[1536,128]{1,0:T(8,128)(2,1)S(1)}, u32[]{:S(2)}, u32[]{:S(2)}) collective-permute-start(bf16[1536,128]{1,0:T(8,128)(2,1)S(1)} %pad_maximum_fusion.1), channel_id=1, source_target_pairs={{0,2},{2,0},{4,6},{6,4},{8,10},{10,8},{12,14},{14,12},{16,18},{18,... | collective-permute-start | bytes 1179656 | tf_op jit(solution)/shard_map/ppermute | solution.py:258
  23.7 0.7 %constant_dynamic-slice_fusion = f32[1,2,16,1,128]{4,2,1,3,0:T(8,128)S(1)} fusion(f32[2,2,16,1,128]{4,2,1,3,0:T(8,128)} %constant.66.clone, s32[]{:T(128)S(6)} %select_n.47), kind=kLoop, calls=%fused_computation.10 | loop fusion | bytes 32772 | tf_op jit(solution)/shard_map/jit(dynamic_index_in_dim)/dynamic_slice | solution.py:280
  24.4 0.1 stack.11
  24.5 0.2 select_reduce_fusion
  24.7 0.1 collective-permute-start.5
  24.8 0.1 collective-permute-start.6
  24.9 5.6 %collective-permute-start.7 = (bf16[768,128]{1,0:T(8,128)(2,1)S(1)}, bf16[768,128]{1,0:T(8,128)(2,1)S(1)}, u32[]{:S(2)}, u32[]{:S(2)}) collective-permute-start(bf16[768,128]{1,0:T(8,128)(2,1)S(1)} %collective-permute-done.2.rest_2_), channel_id=1, source_target_pairs={{0,252},{2,254},{4,0},{6,2},{8,4},{10,6},{12,8},{14,10},{16,12},{1... | collective-permute-start | bytes 589832 | tf_op jit(solution)/shard_map/ppermute | solution.py:254
  30.5 0.0 copy-start
  30.5 0.9 %copy-done = bf16[768,128]{1,0:T(8,128)(2,1)S(1)} copy-done((bf16[768,128]{1,0:T(8,128)(2,1)S(1)}, bf16[768,128]{1,0:T(8,128)(2,1)}, u32[]{:S(2)}) %copy-start) | copy-done | bytes 196632
  31.4 2.0 %turn.1 = (bf16[2048,1536]{1,0:T(8,128)(2,1)S(1)}, f32[128,128]{1,0:T(8,128)S(1)}) custom-call(bf16[768,128]{1,0:T(8,128)(2,1)S(1)} %copy-done, bf16[768,128]{1,0:T(8,128)(2,1)S(1)} %collective-permute-done.other_ref, f32[2,16,1,128]{3,2,1,0:T(1,128)S(1)} %bitcast.7), custom_call_target="tpu_custom_call" | custom-call | tf_op jit(solution)/shard_map/turn/pallas_call | solution.py:212
  33.4 0.0 collective-permute-done.4.rest_1_.rest_3_
  33.4 2.4 %collective-permute-start.8 = (bf16[768,128]{1,0:T(8,128)(2,1)S(1)}, bf16[768,128]{1,0:T(8,128)(2,1)S(1)}, u32[]{:S(2)}, u32[]{:S(2)}) collective-permute-start(bf16[768,128]{1,0:T(8,128)(2,1)S(1)} %collective-permute-done.other_ref), channel_id=1, source_target_pairs={{0,248},{2,250},{4,252},{6,254},{8,0},{10,2},{12,4},{14,6},{16,8},... | collective-permute-start | bytes 589832 | tf_op jit(solution)/shard_map/ppermute | solution.py:254
  35.9 0.0 collective-permute-done.9.rest_1_.rest_2_
  35.9 1.4 %collective-permute-start.10 = (bf16[768,128]{1,0:T(8,128)(2,1)S(1)}, bf16[768,128]{1,0:T(8,128)(2,1)S(1)}, u32[]{:S(2)}, u32[]{:S(2)}) collective-permute-start(bf16[768,128]{1,0:T(8,128)(2,1)S(1)} %slice_select_fusion), channel_id=1, source_target_pairs={{0,2},{2,0},{4,6},{6,4},{8,10},{10,8},{12,14},{14,12},{16,18},{18,... | collective-permute-start | bytes 589832 | tf_op jit(solution)/shard_map/ppermute | solution.py:258
  37.3 0.1 fusion.2
  37.4 3.4 %pair.3.rest_4_ = f32[6,16,128,128]{3,2,1,0:T(8,128)} custom-call(s32[2]{0:T(128)S(1)} %get-tuple-element.21.slot_ref, bf16[2048,1536]{1,0:T(8,128)(2,1)S(1)} %get-tuple-element.17.turned_ref, f32[128,128]{1,0:T(8,128)S(1)} %get-tuple-element.18.scale_ref, bf16[768,128]{1,0:T(8,128)(2,1)S(1)} %collective-permute-done.1.rest_0_, ...), custom_call_target="tpu_custom_call" | custom-call | tf_op jit(solution)/shard_map/pair/pallas_call | solution.py:237
  40.7 0.0 collective-permute-done.10.rest_3_
  40.7 3.4 %pair.4.rest_4_ = f32[6,16,128,128]{3,2,1,0:T(8,128)} custom-call(s32[2]{0:T(128)S(1)} %get-tuple-element.22.slot_ref, bf16[2048,1536]{1,0:T(8,128)(2,1)S(1)} %get-tuple-element.17.turned_ref, f32[128,128]{1,0:T(8,128)S(1)} %get-tuple-element.18.scale_ref, bf16[768,128]{1,0:T(8,128)(2,1)S(1)} %collective-permute-done.3.rest_0_, ...), custom_call_target="tpu_custom_call", output_to_operand_aliasing={{}: (7, {})} | custom-call | tf_op jit(solution)/shard_map/pair/pallas_call | solution.py:237
  44.1 0.0 collective-permute-done.5.rest_0_
  44.1 0.0 collective-permute-done.6.rest_1_
  44.1 0.0 collective-permute-done.7.rest_2_
  44.1 0.1 collective-permute-done.8.rest_3_
  44.2 3.4 %pair.5 = f32[6,16,128,128]{3,2,1,0:T(8,128)} custom-call(s32[2]{0:T(128)S(1)} %get-tuple-element.23.slot_ref, bf16[2048,1536]{1,0:T(8,128)(2,1)S(1)} %get-tuple-element.17.turned_ref, f32[128,128]{1,0:T(8,128)S(1)} %get-tuple-element.18.scale_ref, bf16[768,128]{1,0:T(8,128)(2,1)S(1)} %collective-permute-done.5.rest_0_, ...), custom_call_target="tpu_custom_call", output_to_operand_aliasing={{}: (7, {})} | custom-call | tf_op jit(solution)/shard_map/pair/pallas_call | solution.py:237
  (4 shorter events, 0.1 us)
Async XLA Ops:
  3.6 13.6 %collective-permute-start = (bf16[768,128]{1,0:T(8,128)(2,1)}, bf16[768,128]{1,0:T(8,128)(2,1)S(1)}, u32[]{:S(2)}, u32[]{:S(2)}) collective-permute-start(bf16[768,128]{1,0:T(8,128)(2,1)} %spectra.1.own_ref), channel_id=1, source_target_pairs={{0,1},{1,0},{2,3},{3,2},{4,5},{5,4},{6,7},{7,6},{8,9},{9,8},{10,11... | collective-permute-start | bytes 589832 | tf_op jit(solution)/shard_map/ppermute | solution.py:262
  7.3 12.6 %collective-permute-start.1 = (bf16[768,128]{1,0:T(8,128)(2,1)}, bf16[768,128]{1,0:T(8,128)(2,1)S(1)}, u32[]{:S(2)}, u32[]{:S(2)}) collective-permute-start(bf16[768,128]{1,0:T(8,128)(2,1)} %spectra.1.own_ref), channel_id=1, source_target_pairs={{0,4},{2,6},{4,8},{6,10},{8,12},{10,14},{12,16},{14,18},{16,20},{1... | collective-permute-start | bytes 589832 | tf_op jit(solution)/shard_map/ppermute | solution.py:254
  8.6 11.3 %collective-permute-start.2 = (bf16[768,128]{1,0:T(8,128)(2,1)}, bf16[768,128]{1,0:T(8,128)(2,1)S(1)}, u32[]{:S(2)}, u32[]{:S(2)}) collective-permute-start(bf16[768,128]{1,0:T(8,128)(2,1)} %spectra.1.own_ref), channel_id=1, source_target_pairs={{0,252},{2,254},{4,0},{6,2},{8,4},{10,6},{12,8},{14,10},{16,12},{1... | collective-permute-start | bytes 589832 | tf_op jit(solution)/shard_map/ppermute | solution.py:254
  15.3 4.6 %collective-permute-start.3 = (bf16[768,128]{1,0:T(8,128)(2,1)}, bf16[768,128]{1,0:T(8,128)(2,1)S(1)}, u32[]{:S(2)}, u32[]{:S(2)}) collective-permute-start(bf16[768,128]{1,0:T(8,128)(2,1)} %spectra.1.own_ref), channel_id=1, source_target_pairs={{0,2},{2,0},{4,6},{6,4},{8,10},{10,8},{12,14},{14,12},{16,18},{18,... | collective-permute-start | bytes 589832 | tf_op jit(solution)/shard_map/ppermute | solution.py:258
  19.9 13.5 %collective-permute-start.4 = (bf16[1536,128]{1,0:T(8,128)(2,1)S(1)}, bf16[1536,128]{1,0:T(8,128)(2,1)S(1)}, u32[]{:S(2)}, u32[]{:S(2)}) collective-permute-start(bf16[1536,128]{1,0:T(8,128)(2,1)S(1)} %pad_maximum_fusion), channel_id=1, source_target_pairs={{0,1},{1,0},{2,3},{3,2},{4,5},{5,4},{6,7},{7,6},{8,9},{9,8},{10,11... | collective-permute-start | bytes 1179656 | tf_op jit(solution)/shard_map/ppermute | solution.py:262
  21.8 14.1 %collective-permute-start.9 = (bf16[1536,128]{1,0:T(8,128)(2,1)S(1)}, bf16[1536,128]{1,0:T(8,128)(2,1)S(1)}, u32[]{:S(2)}, u32[]{:S(2)}) collective-permute-start(bf16[1536,128]{1,0:T(8,128)(2,1)S(1)} %pad_maximum_fusion.1), channel_id=1, source_target_pairs={{0,2},{2,0},{4,6},{6,4},{8,10},{10,8},{12,14},{14,12},{16,18},{18,... | collective-permute-start | bytes 1179656 | tf_op jit(solution)/shard_map/ppermute | solution.py:258
  24.7 19.4 %collective-permute-start.5 = (bf16[768,128]{1,0:T(8,128)(2,1)S(1)}, bf16[768,128]{1,0:T(8,128)(2,1)S(1)}, u32[]{:S(2)}, u32[]{:S(2)}) collective-permute-start(bf16[768,128]{1,0:T(8,128)(2,1)S(1)} %collective-permute-done.1.rest_0_), channel_id=1, source_target_pairs={{0,4},{2,6},{4,8},{6,10},{8,12},{10,14},{12,16},{14,18},{16,20},{1... | collective-permute-start | bytes 589832 | tf_op jit(solution)/shard_map/ppermute | solution.py:254
  24.8 19.3 %collective-permute-start.6 = (bf16[768,128]{1,0:T(8,128)(2,1)S(1)}, bf16[768,128]{1,0:T(8,128)(2,1)S(1)}, u32[]{:S(2)}, u32[]{:S(2)}) collective-permute-start(bf16[768,128]{1,0:T(8,128)(2,1)S(1)} %collective-permute-done.other_ref), channel_id=1, source_target_pairs={{0,8},{2,10},{4,12},{6,14},{8,16},{10,18},{12,20},{14,22},{16,24},... | collective-permute-start | bytes 589832 | tf_op jit(solution)/shard_map/ppermute | solution.py:254
  24.9 19.3 %collective-permute-start.7 = (bf16[768,128]{1,0:T(8,128)(2,1)S(1)}, bf16[768,128]{1,0:T(8,128)(2,1)S(1)}, u32[]{:S(2)}, u32[]{:S(2)}) collective-permute-start(bf16[768,128]{1,0:T(8,128)(2,1)S(1)} %collective-permute-done.2.rest_2_), channel_id=1, source_target_pairs={{0,252},{2,254},{4,0},{6,2},{8,4},{10,6},{12,8},{14,10},{16,12},{1... | collective-permute-start | bytes 589832 | tf_op jit(solution)/shard_map/ppermute | solution.py:254
  30.5 0.9 %copy-start = (bf16[768,128]{1,0:T(8,128)(2,1)S(1)}, bf16[768,128]{1,0:T(8,128)(2,1)}, u32[]{:S(2)}) copy-start(bf16[768,128]{1,0:T(8,128)(2,1)} %spectra.1.own_ref) | copy-start | bytes 589828
  33.4 10.8 %collective-permute-start.8 = (bf16[768,128]{1,0:T(8,128)(2,1)S(1)}, bf16[768,128]{1,0:T(8,128)(2,1)S(1)}, u32[]{:S(2)}, u32[]{:S(2)}) collective-permute-start(bf16[768,128]{1,0:T(8,128)(2,1)S(1)} %collective-permute-done.other_ref), channel_id=1, source_target_pairs={{0,248},{2,250},{4,252},{6,254},{8,0},{10,2},{12,4},{14,6},{16,8},... | collective-permute-start | bytes 589832 | tf_op jit(solution)/shard_map/ppermute | solution.py:254
  35.9 4.9 %collective-permute-start.10 = (bf16[768,128]{1,0:T(8,128)(2,1)S(1)}, bf16[768,128]{1,0:T(8,128)(2,1)S(1)}, u32[]{:S(2)}, u32[]{:S(2)}) collective-permute-start(bf16[768,128]{1,0:T(8,128)(2,1)S(1)} %slice_select_fusion), channel_id=1, source_target_pairs={{0,2},{2,0},{4,6},{6,4},{8,10},{10,8},{12,14},{14,12},{16,18},{18,... | collective-permute-start | bytes 589832 | tf_op jit(solution)/shard_map/ppermute | solution.py:258

commit v2 on v1

--- a/solution.py
+++ b/solution.py
@@ -32,41 +32,39 @@
     lag = angles(lag_values[:, None] * bins[None, :], samples)
     lag_table = np.stack([np.cos(lag), np.sin(lag)], axis=0).astype(np.float32)
     lag_table = lag_table.reshape(2, LAGS // half_lags, half_lags, 1, NB).transpose(1, 0, 2, 3, 4)
-    return (
-        dft,
-        np.stack([np.cos(band), -np.sin(band)]).astype(np.float32),
-        np.concatenate([np.cos(white), -np.sin(white)], axis=0).astype(np.float32),
-        lag_table,
-    )
+    taps = np.zeros((2 * NB, -(-(band_count + white_count) // 128) * 128), np.float32)
+    for at, wave in ((0, band), (band_count, white)):
+        taps[:, at : at + wave.shape[1]] = np.concatenate([np.cos(wave), -np.sin(wave)], axis=0)
+    return dft, taps, lag_table
 
 
 def spectra_kernel(
-    rec_hbm, dft_hbm, band_hbm, white_hbm, band_taps, white_taps, live_hbm, out_ref,
-    rec_ref, dft_ref, band_table, white_table, band_ref, white_ref, live_ref, sems, rec_sems,
+    rec_hbm, dft_hbm, table_hbm, band_taps, white_taps, live_hbm, out_ref,
+    rec_ref, dft_ref, table_ref, band_ref, white_ref, live_ref, sems, rec_sems,
 ):
     segments, samples, channels = rec_ref.shape
     small = [
-        (band_hbm, band_table),
-        (white_hbm, white_table),
+        (table_hbm, table_ref),
         (band_taps, band_ref),
         (white_taps, white_ref),
         (live_hbm, live_ref),
-        (dft_hbm, dft_ref),
     ]
     copies = [pltpu.make_async_copy(a, b, sems.at[k]) for k, (a, b) in enumerate(small)]
+    dft_copy = pltpu.make_async_copy(dft_hbm, dft_ref, sems.at[len(small)])
     loads = [
         pltpu.make_async_copy(rec_hbm.at[seg], rec_ref.at[seg], rec_sems.at[seg])
         for seg in range(segments)
     ]
-    for copy in copies + loads:
+    for copy in copies + [dft_copy] + loads:
         copy.start()
     for copy in copies:
         copy.wait()
-    band = band_ref[...]
-    band_real = jnp.sum(band_table[0] * band, axis=1, keepdims=True)
-    band_imag = jnp.sum(band_table[1] * band, axis=1, keepdims=True)
+    band_count = band_ref.shape[1]
+    white_count = white_ref.shape[0]
+    band_sum = jnp.sum(table_ref[:, :band_count] * band_ref[...], axis=1, keepdims=True)
+    band_real, band_imag = band_sum[:NB], band_sum[NB:]
     white = jnp.dot(
-        white_table[...],
+        table_ref[:, band_count : band_count + white_count],
         white_ref[...],
         precision=lax.Precision.HIGHEST,
         preferred_element_type=jnp.float32,
@@ -76,6 +74,7 @@
     resp_real = white_real * band_real - white_imag * band_imag
     resp_imag = white_real * band_imag + white_imag * band_real
     period = dft_ref.shape[1]
+    dft_copy.wait()
     for seg in range(segments):
         loads[seg].wait()
         parts = [rec_ref[seg, k * period : (k + 1) * period, :] for k in range(samples // period)]
@@ -171,21 +170,20 @@
 
 def own_spectra(records, band_taps, white_taps, live_mask, consts):
     segments, samples, channels = records.shape
-    dft, band_table, white_table = consts
+    dft, table = consts
     return pl.pallas_call(
         spectra_kernel,
         out_shape=jax.ShapeDtypeStruct((segments * 2 * NB, channels), jnp.bfloat16),
-        in_specs=[pl.BlockSpec(memory_space=pltpu.HBM)] * 7,
+        in_specs=[pl.BlockSpec(memory_space=pltpu.HBM)] * 6,
         out_specs=VMEM,
         scratch_shapes=[
             pltpu.VMEM(records.shape, records.dtype),
             pltpu.VMEM(dft.shape, dft.dtype),
-            pltpu.VMEM(band_table.shape, jnp.float32),
-            pltpu.VMEM(white_table.shape, jnp.float32),
+            pltpu.VMEM(table.shape, jnp.float32),
             pltpu.VMEM((1, band_taps.shape[0]), jnp.float32),
             pltpu.VMEM(white_taps.shape, jnp.float32),
             pltpu.VMEM((1, channels), jnp.int32),
-            pltpu.SemaphoreType.DMA((6,)),
+            pltpu.SemaphoreType.DMA((5,)),
             pltpu.SemaphoreType.DMA((segments,)),
         ],
         name="spectra",
@@ -198,8 +196,7 @@
     )(
         records,
         dft,
-        band_table,
-        white_table,
+        table,
         band_taps.reshape(1, -1),
         white_taps,
         live_mask.reshape(1, -1),
@@ -258,6 +255,27 @@
     return lax.ppermute(value, "chan", [(s, s ^ 1) for s in range(lax.axis_size("chan"))])
 
 
+def swapped(value, partner):
+    count = lax.axis_size("chan")
+    return lax.ppermute(value, "chan", [(s, partner(s) % count) for s in range(count)])
+
+
+def first_swap(value):
+    return swapped(value, lambda s: s + 2 if s // 2 % 2 == 0 else s - 2)
+
+
+def second_swap(value):
+    return swapped(value, lambda s: s - 2 if s // 2 % 2 == 0 else s + 2)
+
+
+def first_far_swap(value):
+    return swapped(value, lambda s: s + 4 if s // 4 % 2 == 0 else s - 4)
+
+
+def second_far_swap(value):
+    return swapped(value, lambda s: s - 4 if s // 4 % 2 == 0 else s + 4)
+
+
 def mirrored(value):
     return lax.ppermute(value, "tm", [(0, 1), (1, 0)])
 
@@ -267,7 +285,7 @@
     my_block = lax.axis_index("chan")
     block_count = lax.axis_size("chan")
     is_odd = my_block % 2 == 1
-    half = own_spectra(records, band_taps, white_taps, live_mask, consts[:3])
+    half = own_spectra(records, band_taps, white_taps, live_mask, consts[:2])
 
     delta = jnp.mod(partners[:, 0] - my_block + block_count // 2, block_count) - block_count // 2
     inner = jnp.where(is_odd, -1, 1)
@@ -277,7 +295,7 @@
     slots = jnp.sum(
         jnp.where(delta[None, :] == offsets[:, None], rounds[None, :], 0), axis=1
     ).astype(jnp.int32)
-    lag_table = lax.dynamic_index_in_dim(consts[3], lax.axis_index("tm"), 0, keepdims=False)
+    lag_table = lax.dynamic_index_in_dim(consts[2], lax.axis_index("tm"), 0, keepdims=False)
 
     far = mirrored(half)
     low2, high2 = shifted(half, 2), shifted(half, -2)

time: 48 us -> 47.6 us (level)
  no operation moved by 1% of the time
where the time goes in v2:
time: 47.6 us; the launch traced here: 47.4 us
  starting transfers between devices  26.3 us (55%)
  Pallas kernels  15.3 us (32%)
  waiting for transfers between devices  2.76 us (6%)
  local copies, waits for them, and re-layouts  1.8 us (4%)
  other arithmetic  0.95 us (2%)
    ppermute x6, starting transfers between devices, shifted(): lax.ppermute(value, 'chan', [(s, (s + steps) % count) for s in range(coun...  16.2 us
    pallas_call x3, Pallas kernels, pair_sums(): pl.pallas_call(functools.partial(pair_kernel, half, [at for _, at in piec...  10.1 us
    ppermute x2, starting transfers between devices, mirrored(): return lax.ppermute(value, 'tm', [(0, 1), (1, 0)])  5.48 us
    ppermute x3, starting transfers between devices, neighbour(): lax.ppermute(value, 'chan', [(s, s ^ 1) for s in range(lax.axis_size('cha...  4.56 us
    pallas_call x1, Pallas kernels, own_spectra(): pl.pallas_call(spectra_kernel, out_shape=jax.ShapeDtypeStruct((segments *...  3.21 us
    ppermute x6, waiting for transfers between devices, shifted(): lax.ppermute(value, 'chan', [(s, (s + steps) % count) for s in range(coun...  2.75 us
    pallas_call x1, Pallas kernels, turned_rows(): pl.pallas_call(turn_kernel, out_shape=(jax.ShapeDtypeStruct((lag_count *...  1.99 us
  transfers between devices with their start and end apart: 11, of which 2 were waited for; matrix products, arithmetic and copies ran while one was open for 4% of the time, Pallas kernels for 18%

profile of v2, /device:TPU:1, one launch (start us, length us, event | category | flops | bytes accessed | tf_op | source)
XLA Modules:
  0.0 47.4 jit_solution(2571822988824587153)
XLA Ops:
  0.0 3.2 %spectra.1.own_ref = bf16[768,128]{1,0:T(8,128)(2,1)} custom-call(bf16[3,2048,128]{2,1,0:T(8,128)(2,1)} %rec_hbm.1, bf16[256,512]{1,0:T(8,128)(2,1)} %constant.61.clone.dft_hbm, f32[256,128]{1,0:T(8,128)} %constant.62.clone.table_hbm, f32[1,64]{1,0:T(1,128)} %bitcast.8, f32[16,128]{1,0:T(8,128)} %white_taps.1, s32[1,128]{1,0:T(1,128)} %bitcast.9), custom_call_target="tpu_custom_call" | custom-call | flops 402653184 | bytes 1572864 | tf_op jit(solution)/shard_map/spectra/pallas_call | solution.py:174
  3.2 3.7 %collective-permute-start = (bf16[768,128]{1,0:T(8,128)(2,1)}, bf16[768,128]{1,0:T(8,128)(2,1)S(1)}, u32[]{:S(2)}, u32[]{:S(2)}) collective-permute-start(bf16[768,128]{1,0:T(8,128)(2,1)} %spectra.1.own_ref), channel_id=1, source_target_pairs={{0,1},{1,0},{2,3},{3,2},{4,5},{5,4},{6,7},{7,6},{8,9},{9,8},{10,11... | collective-permute-start | bytes 589832 | tf_op jit(solution)/shard_map/ppermute | solution.py:280
  6.9 1.3 %collective-permute-start.1 = (bf16[768,128]{1,0:T(8,128)(2,1)}, bf16[768,128]{1,0:T(8,128)(2,1)S(1)}, u32[]{:S(2)}, u32[]{:S(2)}) collective-permute-start(bf16[768,128]{1,0:T(8,128)(2,1)} %spectra.1.own_ref), channel_id=1, source_target_pairs={{0,4},{2,6},{4,8},{6,10},{8,12},{10,14},{12,16},{14,18},{16,20},{1... | collective-permute-start | bytes 589832 | tf_op jit(solution)/shard_map/ppermute | solution.py:251
  8.2 6.8 %collective-permute-start.2 = (bf16[768,128]{1,0:T(8,128)(2,1)}, bf16[768,128]{1,0:T(8,128)(2,1)S(1)}, u32[]{:S(2)}, u32[]{:S(2)}) collective-permute-start(bf16[768,128]{1,0:T(8,128)(2,1)} %spectra.1.own_ref), channel_id=1, source_target_pairs={{0,252},{2,254},{4,0},{6,2},{8,4},{10,6},{12,8},{14,10},{16,12},{1... | collective-permute-start | bytes 589832 | tf_op jit(solution)/shard_map/ppermute | solution.py:251
  14.9 1.2 %collective-permute-start.3 = (bf16[768,128]{1,0:T(8,128)(2,1)}, bf16[768,128]{1,0:T(8,128)(2,1)S(1)}, u32[]{:S(2)}, u32[]{:S(2)}) collective-permute-start(bf16[768,128]{1,0:T(8,128)(2,1)} %spectra.1.own_ref), channel_id=1, source_target_pairs={{0,2},{2,0},{4,6},{6,4},{8,10},{10,8},{12,14},{14,12},{16,18},{18,... | collective-permute-start | bytes 589832 | tf_op jit(solution)/shard_map/ppermute | solution.py:255
  16.2 0.7 %fusion = s32[6]{0:T(128)S(1)} fusion(s32[6,1]{0,1:T(1,128)} %param.12, s32[]{:T(128)S(6)} %axis_index.23), kind=kLoop, calls=%fused_computation.8 | loop fusion | flops 84 | bytes 52 | tf_op jit(solution)/shard_map/sub | solution.py:290
  16.8 0.0 collective-permute-done.other_ref
  16.8 2.6 %collective-permute-done.1.rest_0_ = bf16[768,128]{1,0:T(8,128)(2,1)S(1)} collective-permute-done((bf16[768,128]{1,0:T(8,128)(2,1)}, bf16[768,128]{1,0:T(8,128)(2,1)S(1)}, u32[]{:S(2)}, u32[]{:S(2)}) %collective-permute-start.1) | collective-permute-done | bytes 196640 | tf_op jit(solution)/shard_map/ppermute | solution.py:251
  19.5 0.0 collective-permute-done.2.rest_2_
  19.5 0.0 collective-permute-done.3.rest_0_
  19.5 1.8 %collective-permute-start.4 = (bf16[1536,128]{1,0:T(8,128)(2,1)S(1)}, bf16[1536,128]{1,0:T(8,128)(2,1)S(1)}, u32[]{:S(2)}, u32[]{:S(2)}) collective-permute-start(bf16[1536,128]{1,0:T(8,128)(2,1)S(1)} %pad_maximum_fusion), channel_id=1, source_target_pairs={{0,1},{1,0},{2,3},{3,2},{4,5},{5,4},{6,7},{7,6},{8,9},{9,8},{10,11... | collective-permute-start | bytes 1179656 | tf_op jit(solution)/shard_map/ppermute | solution.py:280
  21.4 1.9 %collective-permute-start.9 = (bf16[1536,128]{1,0:T(8,128)(2,1)S(1)}, bf16[1536,128]{1,0:T(8,128)(2,1)S(1)}, u32[]{:S(2)}, u32[]{:S(2)}) collective-permute-start(bf16[1536,128]{1,0:T(8,128)(2,1)S(1)} %pad_maximum_fusion.1), channel_id=1, source_target_pairs={{0,2},{2,0},{4,6},{6,4},{8,10},{10,8},{12,14},{14,12},{16,18},{18,... | collective-permute-start | bytes 1179656 | tf_op jit(solution)/shard_map/ppermute | solution.py:255
  23.3 0.7 %constant_dynamic-slice_fusion = f32[1,2,16,1,128]{4,2,1,3,0:T(8,128)S(1)} fusion(f32[2,2,16,1,128]{4,2,1,3,0:T(8,128)} %constant.63.clone, s32[]{:T(128)S(6)} %select_n.47), kind=kLoop, calls=%fused_computation.10 | loop fusion | bytes 32772 | tf_op jit(solution)/shard_map/jit(dynamic_index_in_dim)/dynamic_slice | solution.py:298
  24.0 0.1 stack.11
  24.1 0.2 select_reduce_fusion
  24.3 0.1 collective-permute-start.5
  24.4 0.1 collective-permute-start.6
  24.5 5.6 %collective-permute-start.7 = (bf16[768,128]{1,0:T(8,128)(2,1)S(1)}, bf16[768,128]{1,0:T(8,128)(2,1)S(1)}, u32[]{:S(2)}, u32[]{:S(2)}) collective-permute-start(bf16[768,128]{1,0:T(8,128)(2,1)S(1)} %collective-permute-done.2.rest_2_), channel_id=1, source_target_pairs={{0,252},{2,254},{4,0},{6,2},{8,4},{10,6},{12,8},{14,10},{16,12},{1... | collective-permute-start | bytes 589832 | tf_op jit(solution)/shard_map/ppermute | solution.py:251
  30.1 0.0 copy-start
  30.1 0.9 %copy-done = bf16[768,128]{1,0:T(8,128)(2,1)S(1)} copy-done((bf16[768,128]{1,0:T(8,128)(2,1)S(1)}, bf16[768,128]{1,0:T(8,128)(2,1)}, u32[]{:S(2)}) %copy-start) | copy-done | bytes 196632
  31.0 2.0 %turn.1 = (bf16[2048,1536]{1,0:T(8,128)(2,1)S(1)}, f32[128,128]{1,0:T(8,128)S(1)}) custom-call(bf16[768,128]{1,0:T(8,128)(2,1)S(1)} %copy-done, bf16[768,128]{1,0:T(8,128)(2,1)S(1)} %collective-permute-done.other_ref, f32[2,16,1,128]{3,2,1,0:T(1,128)S(1)} %bitcast.7), custom_call_target="tpu_custom_call" | custom-call | tf_op jit(solution)/shard_map/turn/pallas_call | solution.py:209
  33.0 0.0 collective-permute-done.4.rest_1_.rest_3_
  33.0 2.4 %collective-permute-start.8 = (bf16[768,128]{1,0:T(8,128)(2,1)S(1)}, bf16[768,128]{1,0:T(8,128)(2,1)S(1)}, u32[]{:S(2)}, u32[]{:S(2)}) collective-permute-start(bf16[768,128]{1,0:T(8,128)(2,1)S(1)} %collective-permute-done.other_ref), channel_id=1, source_target_pairs={{0,248},{2,250},{4,252},{6,254},{8,0},{10,2},{12,4},{14,6},{16,8},... | collective-permute-start | bytes 589832 | tf_op jit(solution)/shard_map/ppermute | solution.py:251
  35.5 0.0 collective-permute-done.9.rest_1_.rest_2_
  35.5 1.4 %collective-permute-start.10 = (bf16[768,128]{1,0:T(8,128)(2,1)S(1)}, bf16[768,128]{1,0:T(8,128)(2,1)S(1)}, u32[]{:S(2)}, u32[]{:S(2)}) collective-permute-start(bf16[768,128]{1,0:T(8,128)(2,1)S(1)} %slice_select_fusion), channel_id=1, source_target_pairs={{0,2},{2,0},{4,6},{6,4},{8,10},{10,8},{12,14},{14,12},{16,18},{18,... | collective-permute-start | bytes 589832 | tf_op jit(solution)/shard_map/ppermute | solution.py:255
  36.9 0.1 fusion.2
  37.0 3.4 %pair.3.rest_4_ = f32[6,16,128,128]{3,2,1,0:T(8,128)} custom-call(s32[2]{0:T(128)S(1)} %get-tuple-element.21.slot_ref, bf16[2048,1536]{1,0:T(8,128)(2,1)S(1)} %get-tuple-element.17.turned_ref, f32[128,128]{1,0:T(8,128)S(1)} %get-tuple-element.18.scale_ref, bf16[768,128]{1,0:T(8,128)(2,1)S(1)} %collective-permute-done.1.rest_0_, ...), custom_call_target="tpu_custom_call" | custom-call | tf_op jit(solution)/shard_map/pair/pallas_call | solution.py:234
  40.3 0.0 collective-permute-done.10.rest_3_
  40.3 3.4 %pair.4.rest_4_ = f32[6,16,128,128]{3,2,1,0:T(8,128)} custom-call(s32[2]{0:T(128)S(1)} %get-tuple-element.22.slot_ref, bf16[2048,1536]{1,0:T(8,128)(2,1)S(1)} %get-tuple-element.17.turned_ref, f32[128,128]{1,0:T(8,128)S(1)} %get-tuple-element.18.scale_ref, bf16[768,128]{1,0:T(8,128)(2,1)S(1)} %collective-permute-done.3.rest_0_, ...), custom_call_target="tpu_custom_call", output_to_operand_aliasing={{}: (7, {})} | custom-call | tf_op jit(solution)/shard_map/pair/pallas_call | solution.py:234
  43.7 0.0 collective-permute-done.5.rest_0_
  43.7 0.0 collective-permute-done.6.rest_1_
  43.7 0.0 collective-permute-done.7.rest_2_
  43.7 0.1 collective-permute-done.8.rest_3_
  43.8 3.4 %pair.5 = f32[6,16,128,128]{3,2,1,0:T(8,128)} custom-call(s32[2]{0:T(128)S(1)} %get-tuple-element.23.slot_ref, bf16[2048,1536]{1,0:T(8,128)(2,1)S(1)} %get-tuple-element.17.turned_ref, f32[128,128]{1,0:T(8,128)S(1)} %get-tuple-element.18.scale_ref, bf16[768,128]{1,0:T(8,128)(2,1)S(1)} %collective-permute-done.5.rest_0_, ...), custom_call_target="tpu_custom_call", output_to_operand_aliasing={{}: (7, {})} | custom-call | tf_op jit(solution)/shard_map/pair/pallas_call | solution.py:234
  (4 shorter events, 0.1 us)
Async XLA Ops:
  3.2 13.6 %collective-permute-start = (bf16[768,128]{1,0:T(8,128)(2,1)}, bf16[768,128]{1,0:T(8,128)(2,1)S(1)}, u32[]{:S(2)}, u32[]{:S(2)}) collective-permute-start(bf16[768,128]{1,0:T(8,128)(2,1)} %spectra.1.own_ref), channel_id=1, source_target_pairs={{0,1},{1,0},{2,3},{3,2},{4,5},{5,4},{6,7},{7,6},{8,9},{9,8},{10,11... | collective-permute-start | bytes 589832 | tf_op jit(solution)/shard_map/ppermute | solution.py:280
  6.9 12.6 %collective-permute-start.1 = (bf16[768,128]{1,0:T(8,128)(2,1)}, bf16[768,128]{1,0:T(8,128)(2,1)S(1)}, u32[]{:S(2)}, u32[]{:S(2)}) collective-permute-start(bf16[768,128]{1,0:T(8,128)(2,1)} %spectra.1.own_ref), channel_id=1, source_target_pairs={{0,4},{2,6},{4,8},{6,10},{8,12},{10,14},{12,16},{14,18},{16,20},{1... | collective-permute-start | bytes 589832 | tf_op jit(solution)/shard_map/ppermute | solution.py:251
  8.2 11.3 %collective-permute-start.2 = (bf16[768,128]{1,0:T(8,128)(2,1)}, bf16[768,128]{1,0:T(8,128)(2,1)S(1)}, u32[]{:S(2)}, u32[]{:S(2)}) collective-permute-start(bf16[768,128]{1,0:T(8,128)(2,1)} %spectra.1.own_ref), channel_id=1, source_target_pairs={{0,252},{2,254},{4,0},{6,2},{8,4},{10,6},{12,8},{14,10},{16,12},{1... | collective-permute-start | bytes 589832 | tf_op jit(solution)/shard_map/ppermute | solution.py:251
  14.9 4.6 %collective-permute-start.3 = (bf16[768,128]{1,0:T(8,128)(2,1)}, bf16[768,128]{1,0:T(8,128)(2,1)S(1)}, u32[]{:S(2)}, u32[]{:S(2)}) collective-permute-start(bf16[768,128]{1,0:T(8,128)(2,1)} %spectra.1.own_ref), channel_id=1, source_target_pairs={{0,2},{2,0},{4,6},{6,4},{8,10},{10,8},{12,14},{14,12},{16,18},{18,... | collective-permute-start | bytes 589832 | tf_op jit(solution)/shard_map/ppermute | solution.py:255
  19.5 13.5 %collective-permute-start.4 = (bf16[1536,128]{1,0:T(8,128)(2,1)S(1)}, bf16[1536,128]{1,0:T(8,128)(2,1)S(1)}, u32[]{:S(2)}, u32[]{:S(2)}) collective-permute-start(bf16[1536,128]{1,0:T(8,128)(2,1)S(1)} %pad_maximum_fusion), channel_id=1, source_target_pairs={{0,1},{1,0},{2,3},{3,2},{4,5},{5,4},{6,7},{7,6},{8,9},{9,8},{10,11... | collective-permute-start | bytes 1179656 | tf_op jit(solution)/shard_map/ppermute | solution.py:280
  21.4 14.1 %collective-permute-start.9 = (bf16[1536,128]{1,0:T(8,128)(2,1)S(1)}, bf16[1536,128]{1,0:T(8,128)(2,1)S(1)}, u32[]{:S(2)}, u32[]{:S(2)}) collective-permute-start(bf16[1536,128]{1,0:T(8,128)(2,1)S(1)} %pad_maximum_fusion.1), channel_id=1, source_target_pairs={{0,2},{2,0},{4,6},{6,4},{8,10},{10,8},{12,14},{14,12},{16,18},{18,... | collective-permute-start | bytes 1179656 | tf_op jit(solution)/shard_map/ppermute | solution.py:255
  24.3 19.4 %collective-permute-start.5 = (bf16[768,128]{1,0:T(8,128)(2,1)S(1)}, bf16[768,128]{1,0:T(8,128)(2,1)S(1)}, u32[]{:S(2)}, u32[]{:S(2)}) collective-permute-start(bf16[768,128]{1,0:T(8,128)(2,1)S(1)} %collective-permute-done.1.rest_0_), channel_id=1, source_target_pairs={{0,4},{2,6},{4,8},{6,10},{8,12},{10,14},{12,16},{14,18},{16,20},{1... | collective-permute-start | bytes 589832 | tf_op jit(solution)/shard_map/ppermute | solution.py:251
  24.4 19.3 %collective-permute-start.6 = (bf16[768,128]{1,0:T(8,128)(2,1)S(1)}, bf16[768,128]{1,0:T(8,128)(2,1)S(1)}, u32[]{:S(2)}, u32[]{:S(2)}) collective-permute-start(bf16[768,128]{1,0:T(8,128)(2,1)S(1)} %collective-permute-done.other_ref), channel_id=1, source_target_pairs={{0,8},{2,10},{4,12},{6,14},{8,16},{10,18},{12,20},{14,22},{16,24},... | collective-permute-start | bytes 589832 | tf_op jit(solution)/shard_map/ppermute | solution.py:251
  24.5 19.3 %collective-permute-start.7 = (bf16[768,128]{1,0:T(8,128)(2,1)S(1)}, bf16[768,128]{1,0:T(8,128)(2,1)S(1)}, u32[]{:S(2)}, u32[]{:S(2)}) collective-permute-start(bf16[768,128]{1,0:T(8,128)(2,1)S(1)} %collective-permute-done.2.rest_2_), channel_id=1, source_target_pairs={{0,252},{2,254},{4,0},{6,2},{8,4},{10,6},{12,8},{14,10},{16,12},{1... | collective-permute-start | bytes 589832 | tf_op jit(solution)/shard_map/ppermute | solution.py:251
  30.1 0.9 %copy-start = (bf16[768,128]{1,0:T(8,128)(2,1)S(1)}, bf16[768,128]{1,0:T(8,128)(2,1)}, u32[]{:S(2)}) copy-start(bf16[768,128]{1,0:T(8,128)(2,1)} %spectra.1.own_ref) | copy-start | bytes 589828
  33.0 10.8 %collective-permute-start.8 = (bf16[768,128]{1,0:T(8,128)(2,1)S(1)}, bf16[768,128]{1,0:T(8,128)(2,1)S(1)}, u32[]{:S(2)}, u32[]{:S(2)}) collective-permute-start(bf16[768,128]{1,0:T(8,128)(2,1)S(1)} %collective-permute-done.other_ref), channel_id=1, source_target_pairs={{0,248},{2,250},{4,252},{6,254},{8,0},{10,2},{12,4},{14,6},{16,8},... | collective-permute-start | bytes 589832 | tf_op jit(solution)/shard_map/ppermute | solution.py:251
  35.5 4.9 %collective-permute-start.10 = (bf16[768,128]{1,0:T(8,128)(2,1)S(1)}, bf16[768,128]{1,0:T(8,128)(2,1)S(1)}, u32[]{:S(2)}, u32[]{:S(2)}) collective-permute-start(bf16[768,128]{1,0:T(8,128)(2,1)S(1)} %slice_select_fusion), channel_id=1, source_target_pairs={{0,2},{2,0},{4,6},{6,4},{8,10},{10,8},{12,14},{14,12},{16,18},{18,... | collective-permute-start | bytes 589832 | tf_op jit(solution)/shard_map/ppermute | solution.py:255

commit v3 on v2

--- a/solution.py
+++ b/solution.py
@@ -127,7 +127,16 @@
     return lax.rsqrt(total / (SEG * NB) + 1e-06)
 
 
-def pair_kernel(half, rows_at, slot_ref, turned_ref, scale_ref, *rest):
+def near_kernel(half, rows_at, turned_ref, a_ref, b_ref, out_ref):
+    ah, bh = [ref[at : at + half, :] for ref, at in zip((a_ref, b_ref), rows_at)]
+    near = jnp.concatenate([ah, bh], axis=1)
+    for start in range(0, turned_ref.shape[0], CHUNK):
+        out_ref[start : start + CHUNK, :] = jnp.dot(
+            turned_ref[start : start + CHUNK, :half], near, preferred_element_type=jnp.float32
+        )
+
+
+def pair_kernel(half, rows_at, started, slot_ref, turned_ref, scale_ref, *rest):
     out_ref, stage, sems = rest[-3:]
     channels = scale_ref.shape[0]
     ah, ao, bh, bo = [ref.at[at : at + half] for ref, at in zip(rest[:4], rows_at)]
@@ -138,9 +147,13 @@
     copies = []
     for chunk in range(rows // CHUNK):
         start = chunk * CHUNK
-        totals = jnp.dot(
-            turned_ref[start : start + CHUNK, :half], near, preferred_element_type=jnp.float32
-        ) + jnp.dot(
+        if started:
+            totals = rest[4][start : start + CHUNK, :]
+        else:
+            totals = jnp.dot(
+                turned_ref[start : start + CHUNK, :half], near, preferred_element_type=jnp.float32
+            )
+        totals = totals + jnp.dot(
             turned_ref[start : start + CHUNK, half:], far, preferred_element_type=jnp.float32
         )
         if chunk == 0:
@@ -220,19 +233,34 @@
     )(own, other, lag_table)
 
 
-def pair_sums(slots, turned, scale, first, second, lag_count, previous):
+def near_sums(turned, first, second):
+    half = turned.shape[1] // 2
+    (a, a_at), (b, b_at) = first, second
+    return pl.pallas_call(
+        functools.partial(near_kernel, half, (a_at, b_at)),
+        out_shape=jax.ShapeDtypeStruct((turned.shape[0], 2 * a.shape[1]), jnp.float32),
+        in_specs=[VMEM] * 3,
+        out_specs=VMEM,
+        name="near",
+        compiler_params=pltpu.CompilerParams(vmem_limit_bytes=24 << 20),
+    )(turned, a, b)
+
+
+def pair_sums(slots, turned, scale, first, second, lag_count, previous, partial=None):
     channels = scale.shape[0]
     half = turned.shape[1] // 2
     pieces = [*first, *second]
     operands = [slots, turned, scale] + [array for array, _ in pieces]
-    specs = [pl.BlockSpec(memory_space=pltpu.SMEM)] + [VMEM] * 6
+    if partial is not None:
+        operands.append(partial)
+    specs = [pl.BlockSpec(memory_space=pltpu.SMEM)] + [VMEM] * (len(operands) - 1)
     aliases = {}
     if previous is not None:
         aliases = {len(operands): 0}
         operands.append(previous)
         specs.append(pl.BlockSpec(memory_space=pl.ANY))
     return pl.pallas_call(
-        functools.partial(pair_kernel, half, [at for _, at in pieces]),
+        functools.partial(pair_kernel, half, [at for _, at in pieces], partial is not None),
         out_shape=jax.ShapeDtypeStruct((ROUNDS, lag_count, channels, channels), jnp.float32),
         in_specs=specs,
         out_specs=pl.BlockSpec(memory_space=pl.ANY),
@@ -308,13 +336,14 @@
     turned, scale = turned_rows(half, far, lag_table)
     size = half.shape[0]
     sent = jnp.where(is_odd, both_far[:size], both_far[size:])
-    sent, turned = lax.optimization_barrier((sent, turned))
+    part2 = near_sums(turned, (low2, 0), (high2, 0))
+    sent, turned, part2 = lax.optimization_barrier((sent, turned, part2))
     across_far = neighbour(sent)
 
     near2 = ((low2, 0), (both_far, 0)), ((high2, 0), (both_far, size))
     near1 = ((chip, 0), (mixed, 0)), ((mixed, size), (across_far, 0))
     near4 = ((low4, 0), (low4_far, 0)), ((high4, 0), (high4_far, 0))
-    out = pair_sums(slots[0:2], turned, scale, *near2, lag_count, None)
+    out = pair_sums(slots[0:2], turned, scale, *near2, lag_count, None, part2)
     out = pair_sums(slots[2:4], turned, scale, *near1, lag_count, out)
     return pair_sums(slots[4:6], turned, scale, *near4, lag_count, out)
 

time: 47.6 us -> 51.2 us (1.076)
  starting transfers between devices: 26.3 us -> 29.9 us
    ppermute x6, starting transfers between devices: 16.2 us -> 19.9 us  [shifted(): lax.ppermute(value, 'chan', [(s, (s + steps) % count) for s in range(coun...]
    pallas_call x0 -> x1, Pallas kernels: none -> 0.97 us  [near_sums(): pl.pallas_call(functools.partial(near_kernel, half, (a_at, b_at)), out_sh...]
    pallas_call x3, Pallas kernels: 10.1 us -> 9.26 us  [pair_sums(): pl.pallas_call(functools.partial(pair_kernel, half, [at for _, at in piec...]
  transfers between devices with their start and end apart: 11 -> 11, of which waited for: 2 -> 1; matrix products, arithmetic and copies ran while one was open for 4% -> 4% of each run, Pallas kernels for 18% -> 17%
where the time goes in v3:
time: 51.2 us; the launch traced here: 51 us
  starting transfers between devices  29.9 us (58%)
  Pallas kernels  15.4 us (30%)
  waiting for transfers between devices  2.67 us (5%)
  local copies, waits for them, and re-layouts  1.8 us (4%)
  other arithmetic  0.95 us (2%)
    ppermute x6, starting transfers between devices, shifted(): lax.ppermute(value, 'chan', [(s, (s + steps) % count) for s in range(coun...  19.9 us
    pallas_call x3, Pallas kernels, pair_sums(): pl.pallas_call(functools.partial(pair_kernel, half, [at for _, at in piec...  9.26 us
    ppermute x2, starting transfers between devices, mirrored(): return lax.ppermute(value, 'tm', [(0, 1), (1, 0)])  5.48 us
    ppermute x3, starting transfers between devices, neighbour(): lax.ppermute(value, 'chan', [(s, s ^ 1) for s in range(lax.axis_size('cha...  4.56 us
    pallas_call x1, Pallas kernels, own_spectra(): pl.pallas_call(spectra_kernel, out_shape=jax.ShapeDtypeStruct((segments *...  3.21 us
    ppermute x6, waiting for transfers between devices, shifted(): lax.ppermute(value, 'chan', [(s, (s + steps) % count) for s in range(coun...  2.65 us
    pallas_call x1, Pallas kernels, turned_rows(): pl.pallas_call(turn_kernel, out_shape=(jax.ShapeDtypeStruct((lag_count *...  1.99 us
  transfers between devices with their start and end apart: 11, of which 1 were waited for; matrix products, arithmetic and copies ran while one was open for 4% of the time, Pallas kernels for 17%

profile of v3, /device:TPU:1, one launch (start us, length us, event | category | flops | bytes accessed | tf_op | source)
XLA Modules:
  0.0 51.0 jit_solution(5089669160308270795)
XLA Ops:
  0.0 3.2 %spectra.1.own_ref = bf16[768,128]{1,0:T(8,128)(2,1)} custom-call(bf16[3,2048,128]{2,1,0:T(8,128)(2,1)} %rec_hbm.1, bf16[256,512]{1,0:T(8,128)(2,1)} %constant.61.clone.dft_hbm, f32[256,128]{1,0:T(8,128)} %constant.62.clone.table_hbm, f32[1,64]{1,0:T(1,128)} %bitcast.8, f32[16,128]{1,0:T(8,128)} %white_taps.1, s32[1,128]{1,0:T(1,128)} %bitcast.9), custom_call_target="tpu_custom_call" | custom-call | flops 402653184 | bytes 1572864 | tf_op jit(solution)/shard_map/spectra/pallas_call | solution.py:187
  3.2 3.7 %collective-permute-start = (bf16[768,128]{1,0:T(8,128)(2,1)}, bf16[768,128]{1,0:T(8,128)(2,1)S(1)}, u32[]{:S(2)}, u32[]{:S(2)}) collective-permute-start(bf16[768,128]{1,0:T(8,128)(2,1)} %spectra.1.own_ref), channel_id=1, source_target_pairs={{0,1},{1,0},{2,3},{3,2},{4,5},{5,4},{6,7},{7,6},{8,9},{9,8},{10,11... | collective-permute-start | bytes 589832 | tf_op jit(solution)/shard_map/ppermute | solution.py:308
  6.9 1.3 %collective-permute-start.1 = (bf16[768,128]{1,0:T(8,128)(2,1)}, bf16[768,128]{1,0:T(8,128)(2,1)S(1)}, u32[]{:S(2)}, u32[]{:S(2)}) collective-permute-start(bf16[768,128]{1,0:T(8,128)(2,1)} %spectra.1.own_ref), channel_id=1, source_target_pairs={{0,4},{2,6},{4,8},{6,10},{8,12},{10,14},{12,16},{14,18},{16,20},{1... | collective-permute-start | bytes 589832 | tf_op jit(solution)/shard_map/ppermute | solution.py:279
  8.2 6.8 %collective-permute-start.2 = (bf16[768,128]{1,0:T(8,128)(2,1)}, bf16[768,128]{1,0:T(8,128)(2,1)S(1)}, u32[]{:S(2)}, u32[]{:S(2)}) collective-permute-start(bf16[768,128]{1,0:T(8,128)(2,1)} %spectra.1.own_ref), channel_id=1, source_target_pairs={{0,252},{2,254},{4,0},{6,2},{8,4},{10,6},{12,8},{14,10},{16,12},{1... | collective-permute-start | bytes 589832 | tf_op jit(solution)/shard_map/ppermute | solution.py:279
  14.9 1.2 %collective-permute-start.3 = (bf16[768,128]{1,0:T(8,128)(2,1)}, bf16[768,128]{1,0:T(8,128)(2,1)S(1)}, u32[]{:S(2)}, u32[]{:S(2)}) collective-permute-start(bf16[768,128]{1,0:T(8,128)(2,1)} %spectra.1.own_ref), channel_id=1, source_target_pairs={{0,2},{2,0},{4,6},{6,4},{8,10},{10,8},{12,14},{14,12},{16,18},{18,... | collective-permute-start | bytes 589832 | tf_op jit(solution)/shard_map/ppermute | solution.py:283
  16.2 0.7 %fusion = s32[6]{0:T(128)S(1)} fusion(s32[6,1]{0,1:T(1,128)} %param.12, s32[]{:T(128)S(6)} %axis_index.23), kind=kLoop, calls=%fused_computation.8 | loop fusion | flops 84 | bytes 52 | tf_op jit(solution)/shard_map/sub | solution.py:318
  16.8 0.0 collective-permute-done.other_ref
  16.8 2.6 %collective-permute-done.1.a_ref.rest_0_ = bf16[768,128]{1,0:T(8,128)(2,1)S(1)} collective-permute-done((bf16[768,128]{1,0:T(8,128)(2,1)}, bf16[768,128]{1,0:T(8,128)(2,1)S(1)}, u32[]{:S(2)}, u32[]{:S(2)}) %collective-permute-start.1) | collective-permute-done | bytes 196640 | tf_op jit(solution)/shard_map/ppermute | solution.py:279
  19.5 0.0 collective-permute-done.2.b_ref.rest_2_
  19.5 0.0 collective-permute-done.3.rest_0_
  19.5 1.8 %collective-permute-start.4 = (bf16[1536,128]{1,0:T(8,128)(2,1)S(1)}, bf16[1536,128]{1,0:T(8,128)(2,1)S(1)}, u32[]{:S(2)}, u32[]{:S(2)}) collective-permute-start(bf16[1536,128]{1,0:T(8,128)(2,1)S(1)} %pad_maximum_fusion), channel_id=1, source_target_pairs={{0,1},{1,0},{2,3},{3,2},{4,5},{5,4},{6,7},{7,6},{8,9},{9,8},{10,11... | collective-permute-start | bytes 1179656 | tf_op jit(solution)/shard_map/ppermute | solution.py:308
  21.4 1.9 %collective-permute-start.9 = (bf16[1536,128]{1,0:T(8,128)(2,1)S(1)}, bf16[1536,128]{1,0:T(8,128)(2,1)S(1)}, u32[]{:S(2)}, u32[]{:S(2)}) collective-permute-start(bf16[1536,128]{1,0:T(8,128)(2,1)S(1)} %pad_maximum_fusion.1), channel_id=1, source_target_pairs={{0,2},{2,0},{4,6},{6,4},{8,10},{10,8},{12,14},{14,12},{16,18},{18,... | collective-permute-start | bytes 1179656 | tf_op jit(solution)/shard_map/ppermute | solution.py:283
  23.3 0.7 %constant_dynamic-slice_fusion = f32[1,2,16,1,128]{4,2,1,3,0:T(8,128)S(1)} fusion(f32[2,2,16,1,128]{4,2,1,3,0:T(8,128)} %constant.63.clone, s32[]{:T(128)S(6)} %select_n.47), kind=kLoop, calls=%fused_computation.10 | loop fusion | bytes 32772 | tf_op jit(solution)/shard_map/jit(dynamic_index_in_dim)/dynamic_slice | solution.py:326
  24.0 0.1 stack.11
  24.1 0.2 select_reduce_fusion
  24.3 0.1 collective-permute-start.5
  24.4 5.7 %collective-permute-start.7 = (bf16[768,128]{1,0:T(8,128)(2,1)S(1)}, bf16[768,128]{1,0:T(8,128)(2,1)S(1)}, u32[]{:S(2)}, u32[]{:S(2)}) collective-permute-start(bf16[768,128]{1,0:T(8,128)(2,1)S(1)} %collective-permute-done.2.b_ref.rest_2_), channel_id=1, source_target_pairs={{0,252},{2,254},{4,0},{6,2},{8,4},{10,6},{12,8},{14,10},{16,12},{1... | collective-permute-start | bytes 589832 | tf_op jit(solution)/shard_map/ppermute | solution.py:279
  30.1 0.0 collective-permute-start.6
  30.1 0.0 copy-start
  30.1 0.9 %copy-done = bf16[768,128]{1,0:T(8,128)(2,1)S(1)} copy-done((bf16[768,128]{1,0:T(8,128)(2,1)S(1)}, bf16[768,128]{1,0:T(8,128)(2,1)}, u32[]{:S(2)}) %copy-start) | copy-done | bytes 196632
  31.0 2.0 %turn.1 = (bf16[2048,1536]{1,0:T(8,128)(2,1)S(1)}, f32[128,128]{1,0:T(8,128)S(1)}) custom-call(bf16[768,128]{1,0:T(8,128)(2,1)S(1)} %copy-done, bf16[768,128]{1,0:T(8,128)(2,1)S(1)} %collective-permute-done.other_ref, f32[2,16,1,128]{3,2,1,0:T(1,128)S(1)} %bitcast.7), custom_call_target="tpu_custom_call" | custom-call | tf_op jit(solution)/shard_map/turn/pallas_call | solution.py:222
  33.0 1.0 %near.1.rest_4_ = f32[2048,256]{1,0:T(8,128)S(1)} custom-call(bf16[2048,1536]{1,0:T(8,128)(2,1)S(1)} %get-tuple-element.18.turned_ref, bf16[768,128]{1,0:T(8,128)(2,1)S(1)} %collective-permute-done.1.a_ref.rest_0_, bf16[768,128]{1,0:T(8,128)(2,1)S(1)} %collective-permute-done.2.b_ref.rest_2_), custom_call_target="tpu_custom_call" | custom-call | tf_op jit(solution)/shard_map/near/pallas_call | solution.py:239
  34.0 0.0 collective-permute-done.4.rest_1_.rest_3_
  34.0 6.1 %collective-permute-start.8 = (bf16[768,128]{1,0:T(8,128)(2,1)S(1)}, bf16[768,128]{1,0:T(8,128)(2,1)S(1)}, u32[]{:S(2)}, u32[]{:S(2)}) collective-permute-start(bf16[768,128]{1,0:T(8,128)(2,1)S(1)} %collective-permute-done.other_ref), channel_id=1, source_target_pairs={{0,248},{2,250},{4,252},{6,254},{8,0},{10,2},{12,4},{14,6},{16,8},... | collective-permute-start | bytes 589832 | tf_op jit(solution)/shard_map/ppermute | solution.py:279
  40.1 0.0 collective-permute-done.9.rest_1_.rest_2_
  40.1 1.4 %collective-permute-start.10 = (bf16[768,128]{1,0:T(8,128)(2,1)S(1)}, bf16[768,128]{1,0:T(8,128)(2,1)S(1)}, u32[]{:S(2)}, u32[]{:S(2)}) collective-permute-start(bf16[768,128]{1,0:T(8,128)(2,1)S(1)} %slice_select_fusion), channel_id=1, source_target_pairs={{0,2},{2,0},{4,6},{6,4},{8,10},{10,8},{12,14},{14,12},{16,18},{18,... | collective-permute-start | bytes 589832 | tf_op jit(solution)/shard_map/ppermute | solution.py:283
  41.5 0.1 fusion.2
  41.6 2.5 %pair.3.rest_4_ = f32[6,16,128,128]{3,2,1,0:T(8,128)} custom-call(s32[2]{0:T(128)S(1)} %get-tuple-element.23.slot_ref, bf16[2048,1536]{1,0:T(8,128)(2,1)S(1)} %get-tuple-element.18.turned_ref, f32[128,128]{1,0:T(8,128)S(1)} %get-tuple-element.19.scale_ref, bf16[768,128]{1,0:T(8,128)(2,1)S(1)} %collective-permute-done.1.a_ref.rest_0_, ...), custom_call_target="tpu_custom_call" | custom-call | tf_op jit(solution)/shard_map/pair/pallas_call | solution.py:262
  44.1 0.0 collective-permute-done.10.rest_3_
  44.1 3.4 %pair.4.rest_4_ = f32[6,16,128,128]{3,2,1,0:T(8,128)} custom-call(s32[2]{0:T(128)S(1)} %get-tuple-element.24.slot_ref, bf16[2048,1536]{1,0:T(8,128)(2,1)S(1)} %get-tuple-element.18.turned_ref, f32[128,128]{1,0:T(8,128)S(1)} %get-tuple-element.19.scale_ref, bf16[768,128]{1,0:T(8,128)(2,1)S(1)} %collective-permute-done.3.rest_0_, ...), custom_call_target="tpu_custom_call", output_to_operand_aliasing={{}: (7, {})} | custom-call | tf_op jit(solution)/shard_map/pair/pallas_call | solution.py:262
  47.5 0.0 collective-permute-done.5.rest_0_
  47.5 0.0 collective-permute-done.7.rest_2_
  47.5 0.0 collective-permute-done.6.rest_1_
  47.5 0.0 collective-permute-done.8.rest_3_
  47.5 3.4 %pair.5 = f32[6,16,128,128]{3,2,1,0:T(8,128)} custom-call(s32[2]{0:T(128)S(1)} %get-tuple-element.25.slot_ref, bf16[2048,1536]{1,0:T(8,128)(2,1)S(1)} %get-tuple-element.18.turned_ref, f32[128,128]{1,0:T(8,128)S(1)} %get-tuple-element.19.scale_ref, bf16[768,128]{1,0:T(8,128)(2,1)S(1)} %collective-permute-done.5.rest_0_, ...), custom_call_target="tpu_custom_call", output_to_operand_aliasing={{}: (7, {})} | custom-call | tf_op jit(solution)/shard_map/pair/pallas_call | solution.py:262
  (4 shorter events, 0.1 us)
Async XLA Ops:
  3.2 13.6 %collective-permute-start = (bf16[768,128]{1,0:T(8,128)(2,1)}, bf16[768,128]{1,0:T(8,128)(2,1)S(1)}, u32[]{:S(2)}, u32[]{:S(2)}) collective-permute-start(bf16[768,128]{1,0:T(8,128)(2,1)} %spectra.1.own_ref), channel_id=1, source_target_pairs={{0,1},{1,0},{2,3},{3,2},{4,5},{5,4},{6,7},{7,6},{8,9},{9,8},{10,11... | collective-permute-start | bytes 589832 | tf_op jit(solution)/shard_map/ppermute | solution.py:308
  6.9 12.6 %collective-permute-start.1 = (bf16[768,128]{1,0:T(8,128)(2,1)}, bf16[768,128]{1,0:T(8,128)(2,1)S(1)}, u32[]{:S(2)}, u32[]{:S(2)}) collective-permute-start(bf16[768,128]{1,0:T(8,128)(2,1)} %spectra.1.own_ref), channel_id=1, source_target_pairs={{0,4},{2,6},{4,8},{6,10},{8,12},{10,14},{12,16},{14,18},{16,20},{1... | collective-permute-start | bytes 589832 | tf_op jit(solution)/shard_map/ppermute | solution.py:279
  8.2 11.3 %collective-permute-start.2 = (bf16[768,128]{1,0:T(8,128)(2,1)}, bf16[768,128]{1,0:T(8,128)(2,1)S(1)}, u32[]{:S(2)}, u32[]{:S(2)}) collective-permute-start(bf16[768,128]{1,0:T(8,128)(2,1)} %spectra.1.own_ref), channel_id=1, source_target_pairs={{0,252},{2,254},{4,0},{6,2},{8,4},{10,6},{12,8},{14,10},{16,12},{1... | collective-permute-start | bytes 589832 | tf_op jit(solution)/shard_map/ppermute | solution.py:279
  14.9 4.6 %collective-permute-start.3 = (bf16[768,128]{1,0:T(8,128)(2,1)}, bf16[768,128]{1,0:T(8,128)(2,1)S(1)}, u32[]{:S(2)}, u32[]{:S(2)}) collective-permute-start(bf16[768,128]{1,0:T(8,128)(2,1)} %spectra.1.own_ref), channel_id=1, source_target_pairs={{0,2},{2,0},{4,6},{6,4},{8,10},{10,8},{12,14},{14,12},{16,18},{18,... | collective-permute-start | bytes 589832 | tf_op jit(solution)/shard_map/ppermute | solution.py:283
  19.5 14.5 %collective-permute-start.4 = (bf16[1536,128]{1,0:T(8,128)(2,1)S(1)}, bf16[1536,128]{1,0:T(8,128)(2,1)S(1)}, u32[]{:S(2)}, u32[]{:S(2)}) collective-permute-start(bf16[1536,128]{1,0:T(8,128)(2,1)S(1)} %pad_maximum_fusion), channel_id=1, source_target_pairs={{0,1},{1,0},{2,3},{3,2},{4,5},{5,4},{6,7},{7,6},{8,9},{9,8},{10,11... | collective-permute-start | bytes 1179656 | tf_op jit(solution)/shard_map/ppermute | solution.py:308
  21.4 18.7 %collective-permute-start.9 = (bf16[1536,128]{1,0:T(8,128)(2,1)S(1)}, bf16[1536,128]{1,0:T(8,128)(2,1)S(1)}, u32[]{:S(2)}, u32[]{:S(2)}) collective-permute-start(bf16[1536,128]{1,0:T(8,128)(2,1)S(1)} %pad_maximum_fusion.1), channel_id=1, source_target_pairs={{0,2},{2,0},{4,6},{6,4},{8,10},{10,8},{12,14},{14,12},{16,18},{18,... | collective-permute-start | bytes 1179656 | tf_op jit(solution)/shard_map/ppermute | solution.py:283
  24.3 23.2 %collective-permute-start.5 = (bf16[768,128]{1,0:T(8,128)(2,1)S(1)}, bf16[768,128]{1,0:T(8,128)(2,1)S(1)}, u32[]{:S(2)}, u32[]{:S(2)}) collective-permute-start(bf16[768,128]{1,0:T(8,128)(2,1)S(1)} %collective-permute-done.1.a_ref.rest_0_), channel_id=1, source_target_pairs={{0,4},{2,6},{4,8},{6,10},{8,12},{10,14},{12,16},{14,18},{16,20},{1... | collective-permute-start | bytes 589832 | tf_op jit(solution)/shard_map/ppermute | solution.py:279
  24.4 23.1 %collective-permute-start.7 = (bf16[768,128]{1,0:T(8,128)(2,1)S(1)}, bf16[768,128]{1,0:T(8,128)(2,1)S(1)}, u32[]{:S(2)}, u32[]{:S(2)}) collective-permute-start(bf16[768,128]{1,0:T(8,128)(2,1)S(1)} %collective-permute-done.2.b_ref.rest_2_), channel_id=1, source_target_pairs={{0,252},{2,254},{4,0},{6,2},{8,4},{10,6},{12,8},{14,10},{16,12},{1... | collective-permute-start | bytes 589832 | tf_op jit(solution)/shard_map/ppermute | solution.py:279
  30.1 17.4 %collective-permute-start.6 = (bf16[768,128]{1,0:T(8,128)(2,1)S(1)}, bf16[768,128]{1,0:T(8,128)(2,1)S(1)}, u32[]{:S(2)}, u32[]{:S(2)}) collective-permute-start(bf16[768,128]{1,0:T(8,128)(2,1)S(1)} %collective-permute-done.other_ref), channel_id=1, source_target_pairs={{0,8},{2,10},{4,12},{6,14},{8,16},{10,18},{12,20},{14,22},{16,24},... | collective-permute-start | bytes 589832 | tf_op jit(solution)/shard_map/ppermute | solution.py:279
  30.1 0.9 %copy-start = (bf16[768,128]{1,0:T(8,128)(2,1)S(1)}, bf16[768,128]{1,0:T(8,128)(2,1)}, u32[]{:S(2)}) copy-start(bf16[768,128]{1,0:T(8,128)(2,1)} %spectra.1.own_ref) | copy-start | bytes 589828
  34.0 13.5 %collective-permute-start.8 = (bf16[768,128]{1,0:T(8,128)(2,1)S(1)}, bf16[768,128]{1,0:T(8,128)(2,1)S(1)}, u32[]{:S(2)}, u32[]{:S(2)}) collective-permute-start(bf16[768,128]{1,0:T(8,128)(2,1)S(1)} %collective-permute-done.other_ref), channel_id=1, source_target_pairs={{0,248},{2,250},{4,252},{6,254},{8,0},{10,2},{12,4},{14,6},{16,8},... | collective-permute-start | bytes 589832 | tf_op jit(solution)/shard_map/ppermute | solution.py:279
  40.1 4.0 %collective-permute-start.10 = (bf16[768,128]{1,0:T(8,128)(2,1)S(1)}, bf16[768,128]{1,0:T(8,128)(2,1)S(1)}, u32[]{:S(2)}, u32[]{:S(2)}) collective-permute-start(bf16[768,128]{1,0:T(8,128)(2,1)S(1)} %slice_select_fusion), channel_id=1, source_target_pairs={{0,2},{2,0},{4,6},{6,4},{8,10},{10,8},{12,14},{14,12},{16,18},{18,... | collective-permute-start | bytes 589832 | tf_op jit(solution)/shard_map/ppermute | solution.py:283

commit v4 on v2

--- a/solution.py
+++ b/solution.py
@@ -55,7 +55,7 @@
         pltpu.make_async_copy(rec_hbm.at[seg], rec_ref.at[seg], rec_sems.at[seg])
         for seg in range(segments)
     ]
-    for copy in copies + [dft_copy] + loads:
+    for copy in loads[:1] + copies + [dft_copy] + loads[1:]:
         copy.start()
     for copy in copies:
         copy.wait()

time: 47.6 us -> 47.6 us (level)
  no operation moved by 1% of the time
where the time goes in v4:
time: 47.6 us; the launch traced here: 47.4 us
  starting transfers between devices  26.3 us (55%)
  Pallas kernels  15.3 us (32%)
  waiting for transfers between devices  2.77 us (6%)
  local copies, waits for them, and re-layouts  1.8 us (4%)
  other arithmetic  0.95 us (2%)
    ppermute x6, starting transfers between devices, shifted(): lax.ppermute(value, 'chan', [(s, (s + steps) % count) for s in range(coun...  16.2 us
    pallas_call x3, Pallas kernels, pair_sums(): pl.pallas_call(functools.partial(pair_kernel, half, [at for _, at in piec...  10.1 us
    ppermute x2, starting transfers between devices, mirrored(): return lax.ppermute(value, 'tm', [(0, 1), (1, 0)])  5.47 us
    ppermute x3, starting transfers between devices, neighbour(): lax.ppermute(value, 'chan', [(s, s ^ 1) for s in range(lax.axis_size('cha...  4.56 us
    pallas_call x1, Pallas kernels, own_spectra(): pl.pallas_call(spectra_kernel, out_shape=jax.ShapeDtypeStruct((segments *...  3.21 us
    ppermute x6, waiting for transfers between devices, shifted(): lax.ppermute(value, 'chan', [(s, (s + steps) % count) for s in range(coun...  2.76 us
    pallas_call x1, Pallas kernels, turned_rows(): pl.pallas_call(turn_kernel, out_shape=(jax.ShapeDtypeStruct((lag_count *...  1.99 us
  transfers between devices with their start and end apart: 11, of which 2 were waited for; matrix products, arithmetic and copies ran while one was open for 4% of the time, Pallas kernels for 18%

profile of v4, /device:TPU:1, one launch (start us, length us, event | category | flops | bytes accessed | tf_op | source)
XLA Modules:
  0.0 47.4 jit_solution(14804497615700420776)
XLA Ops:
  0.0 3.2 %spectra.1.own_ref = bf16[768,128]{1,0:T(8,128)(2,1)} custom-call(bf16[3,2048,128]{2,1,0:T(8,128)(2,1)} %rec_hbm.1, bf16[256,512]{1,0:T(8,128)(2,1)} %constant.61.clone.dft_hbm, f32[256,128]{1,0:T(8,128)} %constant.62.clone.table_hbm, f32[1,64]{1,0:T(1,128)} %bitcast.8, f32[16,128]{1,0:T(8,128)} %white_taps.1, s32[1,128]{1,0:T(1,128)} %bitcast.9), custom_call_target="tpu_custom_call" | custom-call | flops 402653184 | bytes 1572864 | tf_op jit(solution)/shard_map/spectra/pallas_call | solution.py:174
  3.2 3.7 %collective-permute-start = (bf16[768,128]{1,0:T(8,128)(2,1)}, bf16[768,128]{1,0:T(8,128)(2,1)S(1)}, u32[]{:S(2)}, u32[]{:S(2)}) collective-permute-start(bf16[768,128]{1,0:T(8,128)(2,1)} %spectra.1.own_ref), channel_id=1, source_target_pairs={{0,1},{1,0},{2,3},{3,2},{4,5},{5,4},{6,7},{7,6},{8,9},{9,8},{10,11... | collective-permute-start | bytes 589832 | tf_op jit(solution)/shard_map/ppermute | solution.py:280
  6.9 1.3 %collective-permute-start.1 = (bf16[768,128]{1,0:T(8,128)(2,1)}, bf16[768,128]{1,0:T(8,128)(2,1)S(1)}, u32[]{:S(2)}, u32[]{:S(2)}) collective-permute-start(bf16[768,128]{1,0:T(8,128)(2,1)} %spectra.1.own_ref), channel_id=1, source_target_pairs={{0,4},{2,6},{4,8},{6,10},{8,12},{10,14},{12,16},{14,18},{16,20},{1... | collective-permute-start | bytes 589832 | tf_op jit(solution)/shard_map/ppermute | solution.py:251
  8.2 6.8 %collective-permute-start.2 = (bf16[768,128]{1,0:T(8,128)(2,1)}, bf16[768,128]{1,0:T(8,128)(2,1)S(1)}, u32[]{:S(2)}, u32[]{:S(2)}) collective-permute-start(bf16[768,128]{1,0:T(8,128)(2,1)} %spectra.1.own_ref), channel_id=1, source_target_pairs={{0,252},{2,254},{4,0},{6,2},{8,4},{10,6},{12,8},{14,10},{16,12},{1... | collective-permute-start | bytes 589832 | tf_op jit(solution)/shard_map/ppermute | solution.py:251
  14.9 1.2 %collective-permute-start.3 = (bf16[768,128]{1,0:T(8,128)(2,1)}, bf16[768,128]{1,0:T(8,128)(2,1)S(1)}, u32[]{:S(2)}, u32[]{:S(2)}) collective-permute-start(bf16[768,128]{1,0:T(8,128)(2,1)} %spectra.1.own_ref), channel_id=1, source_target_pairs={{0,2},{2,0},{4,6},{6,4},{8,10},{10,8},{12,14},{14,12},{16,18},{18,... | collective-permute-start | bytes 589832 | tf_op jit(solution)/shard_map/ppermute | solution.py:255
  16.2 0.7 %fusion = s32[6]{0:T(128)S(1)} fusion(s32[6,1]{0,1:T(1,128)} %param.12, s32[]{:T(128)S(6)} %axis_index.23), kind=kLoop, calls=%fused_computation.8 | loop fusion | flops 84 | bytes 52 | tf_op jit(solution)/shard_map/sub | solution.py:290
  16.8 0.0 collective-permute-done.other_ref
  16.8 2.6 %collective-permute-done.1.rest_0_ = bf16[768,128]{1,0:T(8,128)(2,1)S(1)} collective-permute-done((bf16[768,128]{1,0:T(8,128)(2,1)}, bf16[768,128]{1,0:T(8,128)(2,1)S(1)}, u32[]{:S(2)}, u32[]{:S(2)}) %collective-permute-start.1) | collective-permute-done | bytes 196640 | tf_op jit(solution)/shard_map/ppermute | solution.py:251
  19.5 0.0 collective-permute-done.2.rest_2_
  19.5 0.0 collective-permute-done.3.rest_0_
  19.5 1.8 %collective-permute-start.4 = (bf16[1536,128]{1,0:T(8,128)(2,1)S(1)}, bf16[1536,128]{1,0:T(8,128)(2,1)S(1)}, u32[]{:S(2)}, u32[]{:S(2)}) collective-permute-start(bf16[1536,128]{1,0:T(8,128)(2,1)S(1)} %pad_maximum_fusion), channel_id=1, source_target_pairs={{0,1},{1,0},{2,3},{3,2},{4,5},{5,4},{6,7},{7,6},{8,9},{9,8},{10,11... | collective-permute-start | bytes 1179656 | tf_op jit(solution)/shard_map/ppermute | solution.py:280
  21.4 1.9 %collective-permute-start.9 = (bf16[1536,128]{1,0:T(8,128)(2,1)S(1)}, bf16[1536,128]{1,0:T(8,128)(2,1)S(1)}, u32[]{:S(2)}, u32[]{:S(2)}) collective-permute-start(bf16[1536,128]{1,0:T(8,128)(2,1)S(1)} %pad_maximum_fusion.1), channel_id=1, source_target_pairs={{0,2},{2,0},{4,6},{6,4},{8,10},{10,8},{12,14},{14,12},{16,18},{18,... | collective-permute-start | bytes 1179656 | tf_op jit(solution)/shard_map/ppermute | solution.py:255
  23.3 0.7 %constant_dynamic-slice_fusion = f32[1,2,16,1,128]{4,2,1,3,0:T(8,128)S(1)} fusion(f32[2,2,16,1,128]{4,2,1,3,0:T(8,128)} %constant.63.clone, s32[]{:T(128)S(6)} %select_n.47), kind=kLoop, calls=%fused_computation.10 | loop fusion | bytes 32772 | tf_op jit(solution)/shard_map/jit(dynamic_index_in_dim)/dynamic_slice | solution.py:298
  24.0 0.1 stack.11
  24.1 0.2 select_reduce_fusion
  24.3 0.1 collective-permute-start.5
  24.4 0.1 collective-permute-start.6
  24.5 5.6 %collective-permute-start.7 = (bf16[768,128]{1,0:T(8,128)(2,1)S(1)}, bf16[768,128]{1,0:T(8,128)(2,1)S(1)}, u32[]{:S(2)}, u32[]{:S(2)}) collective-permute-start(bf16[768,128]{1,0:T(8,128)(2,1)S(1)} %collective-permute-done.2.rest_2_), channel_id=1, source_target_pairs={{0,252},{2,254},{4,0},{6,2},{8,4},{10,6},{12,8},{14,10},{16,12},{1... | collective-permute-start | bytes 589832 | tf_op jit(solution)/shard_map/ppermute | solution.py:251
  30.1 0.0 copy-start
  30.1 0.9 %copy-done = bf16[768,128]{1,0:T(8,128)(2,1)S(1)} copy-done((bf16[768,128]{1,0:T(8,128)(2,1)S(1)}, bf16[768,128]{1,0:T(8,128)(2,1)}, u32[]{:S(2)}) %copy-start) | copy-done | bytes 196632
  31.0 2.0 %turn.1 = (bf16[2048,1536]{1,0:T(8,128)(2,1)S(1)}, f32[128,128]{1,0:T(8,128)S(1)}) custom-call(bf16[768,128]{1,0:T(8,128)(2,1)S(1)} %copy-done, bf16[768,128]{1,0:T(8,128)(2,1)S(1)} %collective-permute-done.other_ref, f32[2,16,1,128]{3,2,1,0:T(1,128)S(1)} %bitcast.7), custom_call_target="tpu_custom_call" | custom-call | tf_op jit(solution)/shard_map/turn/pallas_call | solution.py:209
  33.0 0.0 collective-permute-done.4.rest_1_.rest_3_
  33.0 2.4 %collective-permute-start.8 = (bf16[768,128]{1,0:T(8,128)(2,1)S(1)}, bf16[768,128]{1,0:T(8,128)(2,1)S(1)}, u32[]{:S(2)}, u32[]{:S(2)}) collective-permute-start(bf16[768,128]{1,0:T(8,128)(2,1)S(1)} %collective-permute-done.other_ref), channel_id=1, source_target_pairs={{0,248},{2,250},{4,252},{6,254},{8,0},{10,2},{12,4},{14,6},{16,8},... | collective-permute-start | bytes 589832 | tf_op jit(solution)/shard_map/ppermute | solution.py:251
  35.5 0.0 collective-permute-done.9.rest_1_.rest_2_
  35.5 1.4 %collective-permute-start.10 = (bf16[768,128]{1,0:T(8,128)(2,1)S(1)}, bf16[768,128]{1,0:T(8,128)(2,1)S(1)}, u32[]{:S(2)}, u32[]{:S(2)}) collective-permute-start(bf16[768,128]{1,0:T(8,128)(2,1)S(1)} %slice_select_fusion), channel_id=1, source_target_pairs={{0,2},{2,0},{4,6},{6,4},{8,10},{10,8},{12,14},{14,12},{16,18},{18,... | collective-permute-start | bytes 589832 | tf_op jit(solution)/shard_map/ppermute | solution.py:255
  36.9 0.1 fusion.2
  37.0 3.4 %pair.3.rest_4_ = f32[6,16,128,128]{3,2,1,0:T(8,128)} custom-call(s32[2]{0:T(128)S(1)} %get-tuple-element.21.slot_ref, bf16[2048,1536]{1,0:T(8,128)(2,1)S(1)} %get-tuple-element.17.turned_ref, f32[128,128]{1,0:T(8,128)S(1)} %get-tuple-element.18.scale_ref, bf16[768,128]{1,0:T(8,128)(2,1)S(1)} %collective-permute-done.1.rest_0_, ...), custom_call_target="tpu_custom_call" | custom-call | tf_op jit(solution)/shard_map/pair/pallas_call | solution.py:234
  40.3 0.0 collective-permute-done.10.rest_3_
  40.3 3.4 %pair.4.rest_4_ = f32[6,16,128,128]{3,2,1,0:T(8,128)} custom-call(s32[2]{0:T(128)S(1)} %get-tuple-element.22.slot_ref, bf16[2048,1536]{1,0:T(8,128)(2,1)S(1)} %get-tuple-element.17.turned_ref, f32[128,128]{1,0:T(8,128)S(1)} %get-tuple-element.18.scale_ref, bf16[768,128]{1,0:T(8,128)(2,1)S(1)} %collective-permute-done.3.rest_0_, ...), custom_call_target="tpu_custom_call", output_to_operand_aliasing={{}: (7, {})} | custom-call | tf_op jit(solution)/shard_map/pair/pallas_call | solution.py:234
  43.7 0.0 collective-permute-done.5.rest_0_
  43.7 0.0 collective-permute-done.6.rest_1_
  43.7 0.0 collective-permute-done.7.rest_2_
  43.7 0.1 collective-permute-done.8.rest_3_
  43.8 3.4 %pair.5 = f32[6,16,128,128]{3,2,1,0:T(8,128)} custom-call(s32[2]{0:T(128)S(1)} %get-tuple-element.23.slot_ref, bf16[2048,1536]{1,0:T(8,128)(2,1)S(1)} %get-tuple-element.17.turned_ref, f32[128,128]{1,0:T(8,128)S(1)} %get-tuple-element.18.scale_ref, bf16[768,128]{1,0:T(8,128)(2,1)S(1)} %collective-permute-done.5.rest_0_, ...), custom_call_target="tpu_custom_call", output_to_operand_aliasing={{}: (7, {})} | custom-call | tf_op jit(solution)/shard_map/pair/pallas_call | solution.py:234
  (4 shorter events, 0.1 us)
Async XLA Ops:
  3.2 13.6 %collective-permute-start = (bf16[768,128]{1,0:T(8,128)(2,1)}, bf16[768,128]{1,0:T(8,128)(2,1)S(1)}, u32[]{:S(2)}, u32[]{:S(2)}) collective-permute-start(bf16[768,128]{1,0:T(8,128)(2,1)} %spectra.1.own_ref), channel_id=1, source_target_pairs={{0,1},{1,0},{2,3},{3,2},{4,5},{5,4},{6,7},{7,6},{8,9},{9,8},{10,11... | collective-permute-start | bytes 589832 | tf_op jit(solution)/shard_map/ppermute | solution.py:280
  6.9 12.6 %collective-permute-start.1 = (bf16[768,128]{1,0:T(8,128)(2,1)}, bf16[768,128]{1,0:T(8,128)(2,1)S(1)}, u32[]{:S(2)}, u32[]{:S(2)}) collective-permute-start(bf16[768,128]{1,0:T(8,128)(2,1)} %spectra.1.own_ref), channel_id=1, source_target_pairs={{0,4},{2,6},{4,8},{6,10},{8,12},{10,14},{12,16},{14,18},{16,20},{1... | collective-permute-start | bytes 589832 | tf_op jit(solution)/shard_map/ppermute | solution.py:251
  8.2 11.3 %collective-permute-start.2 = (bf16[768,128]{1,0:T(8,128)(2,1)}, bf16[768,128]{1,0:T(8,128)(2,1)S(1)}, u32[]{:S(2)}, u32[]{:S(2)}) collective-permute-start(bf16[768,128]{1,0:T(8,128)(2,1)} %spectra.1.own_ref), channel_id=1, source_target_pairs={{0,252},{2,254},{4,0},{6,2},{8,4},{10,6},{12,8},{14,10},{16,12},{1... | collective-permute-start | bytes 589832 | tf_op jit(solution)/shard_map/ppermute | solution.py:251
  14.9 4.6 %collective-permute-start.3 = (bf16[768,128]{1,0:T(8,128)(2,1)}, bf16[768,128]{1,0:T(8,128)(2,1)S(1)}, u32[]{:S(2)}, u32[]{:S(2)}) collective-permute-start(bf16[768,128]{1,0:T(8,128)(2,1)} %spectra.1.own_ref), channel_id=1, source_target_pairs={{0,2},{2,0},{4,6},{6,4},{8,10},{10,8},{12,14},{14,12},{16,18},{18,... | collective-permute-start | bytes 589832 | tf_op jit(solution)/shard_map/ppermute | solution.py:255
  19.5 13.5 %collective-permute-start.4 = (bf16[1536,128]{1,0:T(8,128)(2,1)S(1)}, bf16[1536,128]{1,0:T(8,128)(2,1)S(1)}, u32[]{:S(2)}, u32[]{:S(2)}) collective-permute-start(bf16[1536,128]{1,0:T(8,128)(2,1)S(1)} %pad_maximum_fusion), channel_id=1, source_target_pairs={{0,1},{1,0},{2,3},{3,2},{4,5},{5,4},{6,7},{7,6},{8,9},{9,8},{10,11... | collective-permute-start | bytes 1179656 | tf_op jit(solution)/shard_map/ppermute | solution.py:280
  21.4 14.1 %collective-permute-start.9 = (bf16[1536,128]{1,0:T(8,128)(2,1)S(1)}, bf16[1536,128]{1,0:T(8,128)(2,1)S(1)}, u32[]{:S(2)}, u32[]{:S(2)}) collective-permute-start(bf16[1536,128]{1,0:T(8,128)(2,1)S(1)} %pad_maximum_fusion.1), channel_id=1, source_target_pairs={{0,2},{2,0},{4,6},{6,4},{8,10},{10,8},{12,14},{14,12},{16,18},{18,... | collective-permute-start | bytes 1179656 | tf_op jit(solution)/shard_map/ppermute | solution.py:255
  24.3 19.4 %collective-permute-start.5 = (bf16[768,128]{1,0:T(8,128)(2,1)S(1)}, bf16[768,128]{1,0:T(8,128)(2,1)S(1)}, u32[]{:S(2)}, u32[]{:S(2)}) collective-permute-start(bf16[768,128]{1,0:T(8,128)(2,1)S(1)} %collective-permute-done.1.rest_0_), channel_id=1, source_target_pairs={{0,4},{2,6},{4,8},{6,10},{8,12},{10,14},{12,16},{14,18},{16,20},{1... | collective-permute-start | bytes 589832 | tf_op jit(solution)/shard_map/ppermute | solution.py:251
  24.4 19.3 %collective-permute-start.6 = (bf16[768,128]{1,0:T(8,128)(2,1)S(1)}, bf16[768,128]{1,0:T(8,128)(2,1)S(1)}, u32[]{:S(2)}, u32[]{:S(2)}) collective-permute-start(bf16[768,128]{1,0:T(8,128)(2,1)S(1)} %collective-permute-done.other_ref), channel_id=1, source_target_pairs={{0,8},{2,10},{4,12},{6,14},{8,16},{10,18},{12,20},{14,22},{16,24},... | collective-permute-start | bytes 589832 | tf_op jit(solution)/shard_map/ppermute | solution.py:251
  24.5 19.2 %collective-permute-start.7 = (bf16[768,128]{1,0:T(8,128)(2,1)S(1)}, bf16[768,128]{1,0:T(8,128)(2,1)S(1)}, u32[]{:S(2)}, u32[]{:S(2)}) collective-permute-start(bf16[768,128]{1,0:T(8,128)(2,1)S(1)} %collective-permute-done.2.rest_2_), channel_id=1, source_target_pairs={{0,252},{2,254},{4,0},{6,2},{8,4},{10,6},{12,8},{14,10},{16,12},{1... | collective-permute-start | bytes 589832 | tf_op jit(solution)/shard_map/ppermute | solution.py:251
  30.1 0.9 %copy-start = (bf16[768,128]{1,0:T(8,128)(2,1)S(1)}, bf16[768,128]{1,0:T(8,128)(2,1)}, u32[]{:S(2)}) copy-start(bf16[768,128]{1,0:T(8,128)(2,1)} %spectra.1.own_ref) | copy-start | bytes 589828
  33.0 10.8 %collective-permute-start.8 = (bf16[768,128]{1,0:T(8,128)(2,1)S(1)}, bf16[768,128]{1,0:T(8,128)(2,1)S(1)}, u32[]{:S(2)}, u32[]{:S(2)}) collective-permute-start(bf16[768,128]{1,0:T(8,128)(2,1)S(1)} %collective-permute-done.other_ref), channel_id=1, source_target_pairs={{0,248},{2,250},{4,252},{6,254},{8,0},{10,2},{12,4},{14,6},{16,8},... | collective-permute-start | bytes 589832 | tf_op jit(solution)/shard_map/ppermute | solution.py:251
  35.5 4.9 %collective-permute-start.10 = (bf16[768,128]{1,0:T(8,128)(2,1)S(1)}, bf16[768,128]{1,0:T(8,128)(2,1)S(1)}, u32[]{:S(2)}, u32[]{:S(2)}) collective-permute-start(bf16[768,128]{1,0:T(8,128)(2,1)S(1)} %slice_select_fusion), channel_id=1, source_target_pairs={{0,2},{2,0},{4,6},{6,4},{8,10},{10,8},{12,14},{14,12},{16,18},{18,... | collective-permute-start | bytes 589832 | tf_op jit(solution)/shard_map/ppermute | solution.py:255
